TPU v7x, 512 devices: a whole 4x8x8 slice. The times are simulated.
512 devices in a mesh: dp: 64 (over x, y_hi, z), tensor: 8 (over y_lo, core).
Axes of the slice: x: 4, y: 8 (y_hi: 2, y_lo: 4; y = y_hi * 4 + y_lo), z: 8, core: 2. Of those that a mesh axis runs over, the one named last changes fastest.
Arguments:
- frames_in: bfloat16 [64, 1024, 1536], P('dp', 'tensor'), may hold values from -6 to 6
- lengths: int32 [64], P('dp'), may hold values from 341 to 1024, as said below
- ln_gain: float32 [1536], replicated, may hold values from 0.5 to 2
- ln_bias: float32 [1536], replicated, may hold values from -3 to 3
- glu_weight: bfloat16 [2, 1536, 1536], P(None, 'tensor'), may hold values from -0.15625 to 0.15625
- conv_kernel: bfloat16 [32, 1536], P(None, 'tensor'), may hold values from -1 to 1
- bn_gain: float32 [1536], P('tensor'), may hold values from 0.5 to 2
- bn_bias: float32 [1536], P('tensor'), may hold values from -3 to 3
- out_weight: bfloat16 [1536, 1536], P('tensor'), may hold values from -0.15625 to 0.15625
Outputs:
- frames_out: bfloat16 [64, 1024, 1536], P('dp', 'tensor')
Inputs may be any that keep to these rules, and one draw needn't show every extreme that they name: `lengths`: each span's length lies between 341 and 1024; some span is full in every draw.
All inputs are finite; a program needn't handle non-finite values.
Results may differ from a plain program's by a relative error of at most 0.0095.
Values may be sent and summed in bfloat16 or wider, within the bound.
A program may use at most 64 MiB of HBM per device.

v0:
```python
import jax
import jax.numpy as jnp
from jax import lax
from jax.sharding import PartitionSpec as P

KERNEL = 32


def layer_norm(rows, gain, bias):
    values = rows.astype(jnp.float32)
    center = jnp.mean(values, axis=-1, keepdims=True)
    spread = jnp.mean((values - center) ** 2, axis=-1, keepdims=True)
    return ((values - center) * lax.rsqrt(spread + 1e-05) * gain + bias).astype(jnp.bfloat16)


def contract_last(left, right):
    return lax.dot_general(
        left, right, (((1,), (1,)), ((), ())), preferred_element_type=jnp.float32
    )


def keep_same(stacked):
    return stacked


def batch_stats(conv, weight_rows, own_count, reduce_fn, spread_fn, bn_gain, bn_bias):
    local_sums = reduce_fn(jnp.sum(conv * weight_rows, axis=0)[None])[0]
    sums, count = lax.psum((local_sums, own_count), "dp")
    mean = sums / count
    mean_wide = spread_fn(mean[None])[0]
    local_squares = reduce_fn(jnp.sum(((conv - mean_wide) * weight_rows) ** 2, axis=0)[None])[0]
    squares = lax.psum(local_squares, "dp")
    var = squares / count
    scale = lax.rsqrt(var + 1e-05) * bn_gain
    wide = spread_fn(jnp.stack([scale, bn_bias]))
    return (mean_wide, wide[0], wide[1])


def per_device(
    frames_in, lengths, ln_gain, ln_bias, glu_weight, conv_kernel, bn_gain, bn_bias, out_weight
):
    rows = frames_in[0]
    width = rows.shape[1]
    chans = glu_weight.shape[1]
    normed = layer_norm(rows, ln_gain, ln_bias)
    own_count = lengths[0].astype(jnp.float32)
    taps = conv_kernel.astype(jnp.float32)
    w_glu = glu_weight.reshape(2 * chans, width)
    proj = contract_last(lax.all_gather(normed, "tensor", axis=0, tiled=True), w_glu)
    glu = (proj[:, :chans] * jax.nn.sigmoid(proj[:, chans:])).astype(jnp.bfloat16)
    total_rows = glu.shape[0]
    valid = jnp.arange(total_rows, dtype=jnp.int32) < lengths[0]
    glu = jnp.where(valid[:, None], glu, jnp.zeros_like(glu)).astype(jnp.float32)
    padded = jnp.pad(glu, ((15, KERNEL - 16), (0, 0)))
    conv = jnp.zeros_like(glu)
    for k in range(KERNEL):
        conv = conv + padded[k : k + total_rows] * taps[k]
    weight_rows = valid.astype(jnp.float32)[:, None]
    mean, scale, shift = batch_stats(
        conv, weight_rows, own_count, keep_same, keep_same, bn_gain, bn_bias
    )
    z = (conv - mean) * scale + shift
    act = (z * jax.nn.sigmoid(z)).astype(jnp.bfloat16)
    partial_cols = contract_last(lax.all_gather(act, "tensor", axis=1, tiled=True), out_weight)
    branch = lax.all_to_all(partial_cols, "tensor", split_axis=0, concat_axis=1, tiled=True)
    return (rows.astype(jnp.float32) + branch).astype(jnp.bfloat16)[None]


def solution(mesh):
    return jax.shard_map(
        per_device,
        mesh=mesh,
        in_specs=(
            P("dp", "tensor", None),
            P("dp"),
            P(),
            P(),
            P(None, "tensor", None),
            P(None, "tensor"),
            P("tensor"),
            P("tensor"),
            P("tensor", None),
        ),
        out_specs=P("dp", "tensor", None),
        check_vma=False,
    )
```

profile of v0, /device:TPU:1, one launch (start us, length us, event | category | flops | bytes accessed | tf_op | source)
XLA Modules:
  0.0 588.3 jit_solution(17581477607968345549)
XLA Ops:
  6.5 1.3 copy.11
  7.9 0.2 convert_reduce_fusion
  8.1 0.2 fusion.65
  8.3 1.9 fusion.68
  10.3 0.0 all-gather.3.cloned.1.call-update
  10.3 0.0 all-gather.5.cloned.1.call-start
  11.0 1.0 fusion.78
  12.0 1.0 fusion.77
  13.0 51.8 %all-gather.3.cloned.1.call-done = bf16[1024,1536]{0,1:T(8,128)(2,1)} async-done(((bf16[128,1536]{0,1:T(8,128)(2,1)}), bf16[1024,1536]{0,1:T(8,128)(2,1)}) %all-gather.3.cloned.1.call-update) | async-done | bytes 3145744 | tf_op jit(solution)/shard_map/all_gather | solution.py:49
  64.8 3.3 fusion.79
  68.1 0.2 select_convert_fusion
  68.3 7.3 %multiply_reduce_fusion.1 = (f32[192]{0:T(256)S(1)}, f32[1024,192]{0,1:T(8,128)S(1)}) fusion(f32[1024]{0:T(1024)S(1)} %get-tuple-element.42, f32[192]{0:T(256)S(1)} %bitcast.100, f32[192]{0:T(256)S(1)} %bitcast.99, f32[192]{0:T(256)S(1)} %bitcast.98, f32[192]{0:T(256)S(1)} %bitcast.97, f32[192]{0:T(256)S(1)} %bitcast.96, f32[192]{0:T(256)S(1)} %bitcast.95, ...), kind=kLoop, calls=%fused_computation.113 | loop fusion | flops 12779328 | bytes 1602304 | tf_op jit(solution)/shard_map/reduce_sum | solution.py:27
  75.7 196.7 %all-reduce.1 = (f32[192]{0:T(256)S(1)}, f32[]{:T(128)}) all-reduce(f32[192]{0:T(256)S(1)} %get-tuple-element.7, f32[]{:T(128)S(6)} %convert_element_type.46), channel_id=1, replica_groups=mesh['dp'=64,'tensor'=8] {'dp'}, use_global_device_ids=true, to_apply=%region_3.4 | all-reduce | flops 193 | bytes 1544 | tf_op jit(solution)/shard_map/psum | solution.py:28
  272.3 0.6 broadcast_divide_fusion
  273.0 0.2 multiply_reduce_fusion
  273.2 187.3 %psum.23 = f32[192]{0:T(256)S(1)} all-reduce(f32[192]{0:T(256)S(1)} %multiply_reduce_fusion), channel_id=1, replica_groups=mesh['dp'=64,'tensor'=8] {'dp'}, use_global_device_ids=true, to_apply=%region_6.7 | all-reduce | flops 192 | bytes 1536 | tf_op jit(solution)/shard_map/psum | solution.py:32
  460.6 0.7 rsqrt_multiply_fusion
  461.3 1.1 multiply_convert_fusion
  462.4 89.8 %all-gather.5.cloned.1.call-done = bf16[1024,1536]{0,1:T(8,128)(2,1)} async-done(((bf16[1024,192]{0,1:T(8,128)(2,1)}), bf16[1024,1536]{0,1:T(8,128)(2,1)}) %all-gather.5.cloned.1.call-update) | async-done | bytes 3145744 | tf_op jit(solution)/shard_map/all_gather | solution.py:64
  552.3 2.9 convolution_bitcast_fusion
  555.1 0.1 copy.16
  555.2 25.2 %all_to_all.19 = f32[8,128,192]{1,2,0:T(8,128)S(1)} all-to-all(f32[8,128,192]{1,2,0:T(8,128)S(1)} %bitcast.68), channel_id=1, replica_groups=mesh['dp'=64,'tensor'=8] {'tensor'}, dimensions={0} | all-to-all | bytes 1572864 | tf_op jit(solution)/shard_map/all_to_all | solution.py:65
  580.4 0.1 fusion.69
  580.5 0.9 copy.13
  (11 shorter events, 0.1 us)
Async XLA Ops:
  6.5 58.3 %copy-start = (bf16[2,192,1536]{2,1,0:T(8,128)(2,1)S(1)}, bf16[2,192,1536]{2,1,0:T(8,128)(2,1)}, u32[]{:S(2)}) copy-start(bf16[2,192,1536]{2,1,0:T(8,128)(2,1)} %param.13) | copy-start | bytes 3538948
  6.5 58.3 %all-gather.3.cloned.1.call-start = ((), (), s32[]{:S(2)}) async-start(), calls=%async_computation.1 | async-start | bytes 3538944 | tf_op jit(solution)/shard_map/all_gather | solution.py:49
  10.3 542.0 %all-gather.5.cloned.1.call-start = ((), (), s32[]{:S(2)}) async-start(), calls=%async_computation.2 | async-start | bytes 3538944 | tf_op jit(solution)/shard_map/all_gather | solution.py:64
  68.1 392.5 %copy-start.1 = (f32[192]{0:T(256)S(1)}, f32[192]{0:T(256)}, u32[]{:S(2)}) copy-start(f32[192]{0:T(256)} %param.15) | copy-start | bytes 2308
  68.1 393.2 %copy-start.2 = (f32[192]{0:T(256)S(1)}, f32[192]{0:T(256)}, u32[]{:S(2)}) copy-start(f32[192]{0:T(256)} %param.16) | copy-start | bytes 2308
Sparse Core Ops, SparseCore 0:
  10.4 54.3 all-gather.2
  462.5 89.6 all-gather.4
where the time goes:
time: 589 us; the launch traced here: 588 us
  blocking collectives  409 us (69%)
  waiting for transfers between devices  142 us (24%)
  between operations  14.2 us (2%)
  other arithmetic  12.7 us (2%)
  matrix products  6.12 us (1%)
    psum x1, blocking collectives, batch_stats(): sums, count = lax.psum((local_sums, own_count), 'dp')  197 us
    psum x1, blocking collectives, batch_stats(): squares = lax.psum(local_squares, 'dp')  187 us
    all_gather x1, waiting for transfers between devices, per_device(): lax.all_gather(act, 'tensor', axis=1, tiled=True)  89.8 us
    all_gather x1, waiting for transfers between devices, per_device(): lax.all_gather(normed, 'tensor', axis=0, tiled=True)  51.8 us
    all_to_all x1, blocking collectives, per_device(): lax.all_to_all(partial_cols, 'tensor', split_axis=0, concat_axis=1, tiled...  25.2 us
  transfers between devices with their start and end apart: 2, of which 2 were waited for; matrix products, arithmetic and copies ran while one was open for 0% of the time, Pallas kernels for 0%

commit v1 on v0

v1 whole, which is shorter than its diff:
```python
import functools

import jax
import jax.numpy as jnp
from jax import lax
from jax.experimental import pallas as pl
from jax.experimental.pallas import tpu as pltpu
from jax.sharding import PartitionSpec as P

MESH = pl.DeviceIdType.MESH
F32 = jnp.float32
BF16 = jnp.bfloat16
TAPS = 32
D = 1536
SHARD = 192
CHIP = 384
ROWS = 128
HALO = 16
SPAN = 2 * ROWS
WIN = SPAN + 2 * HALO
PIECES = 3
PROWS = SHARD // PIECES
WCH = 6
WROWS = SHARD // WCH

NAMES = (
    ["glu_sib"]
    + [f"glu_x{i}" for i in range(PIECES)]
    + [f"glu_f{i}" for i in range(PIECES)]
    + ["blk0", "blk1", "low", "high"]
    + ["pack_s", "pack_e", "pack_d"]
    + ["w_sib", "w_par", "w_fp"]
    + [f"w_e{i}" for i in range(WCH)]
    + [f"w_ep{i}" for i in range(WCH)]
    + [f"w_fe{i}" for i in range(WCH)]
    + [f"w_fep{i}" for i in range(WCH)]
    + [f"d{k}_{g}" for k in range(3) for g in range(2)]
    + ["ml0", "ml1"]
)
SEM = {name: i for i, name in enumerate(NAMES)}
SENDS = NAMES + ["blk_s", "blk_p", "low1", "high1"]
SSEM = {name: i for i, name in enumerate(SENDS)}


def body(
    frames, lengths, ln_gain, ln_bias, glu_w, taps_in, bn_gain, bn_bias, out_w, out,
    xin, lng, lnb, tin, bg, bb, own, nbuf, wg, wf, pack, par, gs, cv, dsend, dbuf,
    msg, plane, bmsg, gmsg, ball, gall, mlx, act,
    lsem, ssem, rsem, asend, arecv, bsend, brecv, gsend, grecv,
):
    dp = lax.axis_index("dp")
    t = lax.axis_index("tensor")
    x, yh, z = dp // 16, (dp // 8) % 2, dp % 8
    y, c = t // 2, t % 2
    h, j = y // 2, y % 2
    me = yh * 8 + t
    sib = t + 1 - 2 * c
    par_t = (y + 1 - 2 * j) * 2 + c
    ext_t = (3 - y) * 2 + c
    ext_s = (3 - y) * 2 + 1 - c
    edge = (y == 0) | (y == 3)
    ext_dp = jnp.where(edge, dp + 8 - 16 * yh, dp)
    pe_t = (3 - (y + 1 - 2 * j)) * 2 + c

    def rcopy(src, dst, send, recv, tensor, to_dp=dp):
        return pltpu.make_async_remote_copy(
            src_ref=src, dst_ref=dst, send_sem=ssem.at[SSEM[send]], recv_sem=rsem.at[SEM[recv]],
            device_id={"dp": to_dp, "tensor": tensor}, device_id_type=MESH,
        )

    def arrived(dst, recv):
        pltpu.make_async_remote_copy(
            src_ref=dst, dst_ref=dst, send_sem=ssem.at[0], recv_sem=rsem.at[SEM[recv]],
            device_id={"dp": dp, "tensor": sib}, device_id_type=MESH,
        ).wait_recv()

    barrier = pltpu.get_barrier_semaphore()

    def greet_plane(i, _):
        to = (((x + i // 8) % 4) * 2 + yh) * 8 + (z + i % 8) % 8
        pl.semaphore_signal(barrier, inc=1, device_id={"dp": to, "tensor": t}, device_id_type=MESH)
        return 0

    def greet_line(i, _):
        q = (me + i) % 16
        to = (x * 2 + q // 8) * 8 + z
        pl.semaphore_signal(barrier, inc=1, device_id={"dp": to, "tensor": q % 8}, device_id_type=MESH)
        return 0

    lax.fori_loop(1, 16, greet_line, 0)
    lax.fori_loop(1, 32, greet_plane, 0)

    loads = [
        pltpu.make_async_copy(frames.at[0], xin, lsem.at[0]),
        pltpu.make_async_copy(ln_gain, lng, lsem.at[1]),
        pltpu.make_async_copy(ln_bias, lnb, lsem.at[2]),
        pltpu.make_async_copy(taps_in, tin, lsem.at[3]),
        pltpu.make_async_copy(bn_gain, bg, lsem.at[4]),
        pltpu.make_async_copy(bn_bias, bb, lsem.at[5]),
        pltpu.make_async_copy(glu_w, wg.at[h, :, pl.ds(pl.multiple_of(SHARD * c, 64), SHARD)], lsem.at[6]),
        pltpu.make_async_copy(out_w, wf.at[pl.ds(pl.multiple_of(SHARD * t, 64), SHARD)], lsem.at[7]),
    ]
    for copy in loads:
        copy.start()
    for copy in loads[:6]:
        copy.wait()

    rows = xin[...].astype(F32)
    center = jnp.mean(rows, axis=-1, keepdims=True)
    spread = jnp.mean((rows - center) ** 2, axis=-1, keepdims=True)
    own[...] = ((rows - center) * lax.rsqrt(spread + 1e-05) * lng[...] + lnb[...]).astype(BF16)

    pack[0] = jnp.zeros_like(pack[0])
    pack[0, 0:TAPS, 0:SHARD] = tin[...].astype(F32)
    pack[0, TAPS : TAPS + 1, 0:SHARD] = bg[...]
    pack[0, TAPS + 1 : TAPS + 2, 0:SHARD] = bb[...]

    same = (y + 2 * c - 1) // 2 == h
    gives = ((c == 1) & (y < 3)) | ((c == 0) & (y > 0))
    y2 = y + 2 * c - 1
    h2, j2 = y2 // 2, (y2 + 2) % 2
    mine = j == c

    @pl.when(mine)
    def _():
        nbuf[pl.ds(pl.multiple_of(HALO + ROWS * c, 16), ROWS), :] = own[...]

    @pl.when((c == 1) & (j == 0))
    def _():
        nbuf[0:HALO, :] = own[ROWS - HALO : ROWS, :]

    @pl.when((c == 0) & (j == 1))
    def _():
        nbuf[WIN - HALO : WIN, :] = own[0:HALO, :]

    @pl.when((c == 0) & (h == 0))
    def _():
        nbuf[0:HALO, :] = jnp.zeros((HALO, D), BF16)

    @pl.when((c == 1) & (h == 1))
    def _():
        nbuf[WIN - HALO : WIN, :] = jnp.zeros((HALO, D), BF16)

    pl.semaphore_wait(barrier, 46)

    def glu_rows(slot, core, i):
        first = SHARD * core + PROWS * jnp.where(core == 0, i, PIECES - 1 - i)
        return wg.at[slot, :, pl.ds(pl.multiple_of(first, 64), PROWS)]

    glu_x = []
    for i in range(PIECES):
        first = PROWS * jnp.where(c == 0, i, PIECES - 1 - i)
        src = glu_w.at[:, pl.ds(pl.multiple_of(first, 64), PROWS)]
        glu_x.append(rcopy(src, glu_rows(h, c, i), f"glu_x{i}", f"glu_x{i}", ext_t, ext_dp))
        glu_x[-1].start()

    spot = nbuf.at[pl.ds(pl.multiple_of(HALO + ROWS * c, 16), ROWS)]

    def block_to(send, tensor):
        return (
            rcopy(own, spot, send, "blk0", tensor),
            rcopy(own, spot, send, "blk1", tensor),
        )

    to_partner = block_to("blk_p", (y + 1 - 2 * j) * 2 + j)
    to_sibling = block_to("blk_s", sib)
    for core in range(2):
        pl.when(c == core)(to_partner[core].start)
        pl.when((c == core) & jnp.logical_not(mine))(to_sibling[core].start)

    low = nbuf.at[0:HALO]
    high = nbuf.at[WIN - HALO : WIN]
    tail = own.at[ROWS - HALO : ROWS]
    head = own.at[0:HALO]
    halo_a = jnp.where(same, par_t, (2 * h2) * 2 + j2)
    halo_b = (2 * h2 + 1) * 2 + j2
    halos = [
        ((c == 1) & gives, rcopy(tail, low, "low", "low", halo_a)),
        ((c == 1) & gives & jnp.logical_not(same), rcopy(tail, low, "low1", "low", halo_b)),
        ((c == 0) & gives, rcopy(head, high, "high", "high", halo_a)),
        ((c == 0) & gives & jnp.logical_not(same), rcopy(head, high, "high1", "high", halo_b)),
    ]
    for cond, copy in halos:
        pl.when(cond)(copy.start)

    glu_sib = rcopy(
        glu_w, wg.at[h, :, pl.ds(pl.multiple_of(SHARD * c, 64), SHARD)], "glu_sib", "glu_sib", sib
    )
    glu_sib.start()
    packs = [
        rcopy(pack.at[0], pack.at[1], "pack_s", "pack_s", sib),
        rcopy(pack.at[0], pack.at[2], "pack_e", "pack_e", ext_t, ext_dp),
        rcopy(pack.at[0], pack.at[3], "pack_d", "pack_d", ext_s, ext_dp),
    ]
    for copy in packs:
        copy.start()

    def w_rows(shard, first=0, n=SHARD):
        return wf.at[pl.ds(pl.multiple_of(SHARD * shard + first, 32), n)]

    w_sib = rcopy(out_w, w_rows(t), "w_sib", "w_sib", sib)
    w_sib.start()

    lane = lax.broadcasted_iota(jnp.int32, (40, 128), 1)

    def tiles_of(slot, mine_at, other_at):
        a = pack[mine_at]
        b = pack[other_at]
        first = jnp.where(c == 0, a, b)
        second = jnp.where(c == 0, b, a)
        r0 = pltpu.roll(second[:, 0:128], 64, 1)
        r1 = pltpu.roll(second[:, 128:256], 64, 1)
        par[3 * slot] = first[:, 0:128]
        par[3 * slot + 1] = jnp.where(lane < 64, first[:, 128:256], r0)
        par[3 * slot + 2] = jnp.where(lane < 64, r0, r1)

    arrived(pack.at[1], "pack_s")
    tiles_of(h, 0, 1)
    arrived(pack.at[2], "pack_e")
    arrived(pack.at[3], "pack_d")
    tiles_of(1 - h, 2, 3)
    gmsg[...] = jnp.zeros_like(gmsg)
    for k in range(6):
        gmsg[k : k + 1, :] = par[k, TAPS : TAPS + 1, :]
        gmsg[8 + k : 9 + k, :] = par[k, TAPS + 1 : TAPS + 2, :]

    def line(i, src, dst, ss, rs):
        q = (me + i) % 16
        to = (x * 2 + q // 8) * 8 + z
        return pltpu.make_async_remote_copy(
            src_ref=src, dst_ref=dst.at[me], send_sem=ss.at[i], recv_sem=rs.at[me],
            device_id={"dp": to, "tensor": q % 8}, device_id_type=MESH,
        )

    def send_gains(i, _):
        line(i, gmsg, gall, gsend, grecv).start()
        return 0

    lax.fori_loop(1, 16, send_gains, 0)

    length = lengths[0]
    start = 2 * SPAN * h + SPAN * c
    count = jnp.clip(length - start, 0, SPAN)
    count_f = count.astype(F32)
    inverse = 1.0 / jnp.maximum(count_f, 1.0)
    msg[...] = jnp.zeros_like(msg)
    msg[6:7, :] = jnp.full((1, 128), count_f, F32)

    def one_tile(slot, q):
        k = 3 * slot + q
        w = wg[slot, :, pl.ds(pl.multiple_of(128 * q, 128), 128), :].reshape(256, D)
        both = lax.dot_general(nbuf[...], w, (((1,), (1,)), ((), ())), preferred_element_type=F32)
        glu = (both[:, 0:128] * jax.nn.sigmoid(both[:, 128:256])).astype(BF16).astype(F32)
        at = lax.broadcasted_iota(jnp.int32, (WIN, 128), 0)
        gs[...] = jnp.where(at < length - start + HALO, glu, 0.0)
        step = 64

        def conv_rows(i, total):
            first = pl.multiple_of(i * step, step)
            acc = jnp.zeros((step, 128), F32)
            for tap in range(TAPS):
                acc = acc + gs[pl.ds(first + (tap + 1), step), :] * par[k, tap : tap + 1, :]
            cv[pl.ds(first, step), :] = acc
            here = first + lax.broadcasted_iota(jnp.int32, (step, 128), 0)
            kept = jnp.where(here < count, acc, 0.0)
            return total + jnp.sum(kept.reshape(step // 8, 8, 128), axis=0)

        total = lax.fori_loop(0, SPAN // step, conv_rows, jnp.zeros((8, 128), F32))
        local = jnp.sum(total, axis=0, keepdims=True) * inverse
        dev = cv[...] - local
        dsend[k] = dev.astype(BF16)
        here = lax.broadcasted_iota(jnp.int32, (SPAN, 128), 0)
        kept = jnp.where(here < count, dev, 0.0)
        msg[pl.ds(k, 1), :] = local
        msg[pl.ds(8 + k, 1), :] = jnp.sum(kept * kept, axis=0, keepdims=True)

    owner = 2 * (2 * h + c)
    shard_of = (jnp.minimum(y, 3 - y), jnp.maximum(y, 3 - y))

    def give(slot, q, n, group):
        base = 3 * jnp.where(slot == 0, shard_of[0], shard_of[1]) + q
        copies = []
        for g in range(2):
            src = dsend.at[pl.ds(3 * slot + q, n), pl.ds(ROWS * g, ROWS)]
            dst = dbuf.at[pl.ds(base, n)]
            name = f"d{group}_{g}"
            away = [
                (jnp.logical_not(mine & (c == g)) & (j == s),
                 rcopy(src, dst, name, f"d{group}_{s}", owner + g))
                for s in range(2)
            ]
            for cond, copy in away:
                pl.when(cond)(copy.start)
                copies.append((cond, copy))

            @pl.when(mine & (c == g))
            def _(src=src, dst=dst):
                keep = pltpu.make_async_copy(src, dst, lsem.at[8])
                keep.start()
                keep.wait()
        return copies

    for p in range(2):
        @pl.when(jnp.logical_not(mine & (c == p)))
        def _(p=p):
            arrived(nbuf.at[HALO + ROWS * p : HALO + ROWS * (p + 1)], f"blk{p}")

    @pl.when(((c == 1) & (j == 1)) | ((c == 0) & (h == 1)))
    def _():
        arrived(low, "low")

    @pl.when(((c == 0) & (j == 0)) | ((c == 1) & (h == 0)))
    def _():
        arrived(high, "high")

    loads[6].wait()
    arrived(wg.at[h, :, pl.ds(pl.multiple_of(SHARD * (1 - c), 64), SHARD)], "glu_sib")

    w_par = rcopy(out_w, w_rows(t), "w_par", "w_par", par_t)
    w_par.start()

    def own_tile(q, _):
        one_tile(h, q)
        return 0

    lax.fori_loop(0, 3, own_tile, 0)
    given = give(h, 0, 3, 0)

    glu_f = []
    for i in range(2):
        arrived(glu_rows(1 - h, c, i), f"glu_x{i}")
        glu_f.append(rcopy(glu_rows(1 - h, c, i), glu_rows(1 - h, c, i), f"glu_f{i}", f"glu_f{i}", sib))
        glu_f[-1].start()
    for i in range(2):
        arrived(glu_rows(1 - h, 1 - c, i), f"glu_f{i}")

    def extra_tile(i, _):
        one_tile(1 - h, 2 * i)
        return 0

    lax.fori_loop(0, 2, extra_tile, 0)
    given += give(1 - h, 0, 1, 1)
    arrived(w_rows(par_t), "w_par")
    w_fp = rcopy(w_rows(par_t), w_rows(par_t), "w_fp", "w_fp", sib)
    w_fp.start()

    arrived(glu_rows(1 - h, c, 2), "glu_x2")
    glu_f.append(rcopy(glu_rows(1 - h, c, 2), glu_rows(1 - h, c, 2), "glu_f2", "glu_f2", sib))
    glu_f[-1].start()
    w_e = []
    for i in range(WCH):
        w_e.append(rcopy(
            out_w.at[pl.ds(WROWS * i, WROWS)], w_rows(t, WROWS * i, WROWS), f"w_e{i}", f"w_e{i}", ext_t, ext_dp
        ))
        w_e[-1].start()
    arrived(glu_rows(1 - h, 1 - c, 2), "glu_f2")
    one_tile(1 - h, 1)

    def plane_copy(i):
        to = (((x + i // 8) % 4) * 2 + yh) * 8 + (z + i % 8) % 8
        return pltpu.make_async_remote_copy(
            src_ref=msg, dst_ref=plane.at[i], send_sem=asend.at[i], recv_sem=arecv.at[i],
            device_id={"dp": to, "tensor": t}, device_id_type=MESH,
        )

    def send_plane(i, _):
        plane_copy(i).start()
        return 0

    lax.fori_loop(1, 32, send_plane, 0)
    given += give(1 - h, 1, 2, 2)
    u = jnp.where(edge, 0, 1)
    means = []
    for g in range(2):
        away = [
            (jnp.logical_not(mine & (c == g)) & (u == s),
             rcopy(msg.at[0:8], mlx.at[s], f"ml{g}", f"ml{s}", owner + g))
            for s in range(2)
        ]
        for cond, copy in away:
            pl.when(cond)(copy.start)
            means.append((cond, copy))

    @pl.when(mine)
    def _():
        mlx[u] = msg[0:8, :]

    w_fwd = []

    def forward(i):
        at = w_rows(ext_t, WROWS * i, WROWS)
        arrived(at, f"w_e{i}")
        for name, to in ((f"w_ep{i}", par_t), (f"w_fe{i}", sib)):
            copy = rcopy(at, at, name, name, to)
            copy.start()
            w_fwd.append(copy)

    def forward_again(i):
        at = w_rows(pe_t, WROWS * i, WROWS)
        arrived(at, f"w_ep{i}")
        copy = rcopy(at, at, f"w_fep{i}", f"w_fep{i}", sib)
        copy.start()
        w_fwd.append(copy)

    def merge(blocks):
        n = sum(jnp.broadcast_to(b[6:7, :], (8, 128)) for b in blocks)
        weighted = sum(jnp.broadcast_to(b[6:7, :], (8, 128)) * b[0:8, :] for b in blocks)
        mean = weighted / jnp.maximum(n, 1.0)
        square = sum(
            b[8:16, :] + jnp.broadcast_to(b[6:7, :], (8, 128)) * (b[0:8, :] - mean) ** 2 for b in blocks
        )
        return n, mean, square

    for i in range(3):
        forward(i)

    def wait_plane(i, _):
        plane_copy(i).wait_recv()
        return 0

    lax.fori_loop(1, 32, wait_plane, 0)
    plane[0] = msg[...]
    n, mean, square = merge([plane[i] for i in range(32)])
    row = lax.broadcasted_iota(jnp.int32, (8, 128), 0)
    bmsg[0:8, :] = jnp.where(row == 6, n, mean)
    bmsg[8:16, :] = square

    def send_line(i, _):
        line(i, bmsg, ball, bsend, brecv).start()
        return 0

    lax.fori_loop(1, 16, send_line, 0)
    ball[me] = bmsg[...]
    gall[me] = gmsg[...]

    for i in range(3, WCH):
        forward(i)
        forward_again(i - 3)

    def wait_line(i, _):
        q = (me + i) % 16
        for dst, rs in ((ball, brecv), (gall, grecv)):
            pltpu.make_async_remote_copy(
                src_ref=bmsg, dst_ref=dst.at[q], send_sem=bsend.at[0], recv_sem=rs.at[q],
                device_id={"dp": dp, "tensor": sib}, device_id_type=MESH,
            ).wait_recv()
        return 0

    lax.fori_loop(1, 16, wait_line, 0)

    for group, n in ((0, 3), (1, 1), (2, 2)):
        for s in range(2):
            @pl.when(jnp.logical_not((j == s) & mine))
            def _(group=group, n=n, s=s):
                arrived(dbuf.at[pl.ds(0, n)], f"d{group}_{s}")
    for s in range(2):
        @pl.when(jnp.logical_not((u == s) & mine))
        def _(s=s):
            arrived(mlx.at[s], f"ml{s}")

    sets = ((0, 1, 6, 7), (2, 3, 4, 5))
    offset, scale, shift = [], [], []
    for s in range(2):
        n, mean, square = merge([ball[8 * g + q] for g in range(2) for q in sets[s]])
        n1 = jnp.broadcast_to(n[0:1, :], (8, 128))
        gains = gall[sets[s][0]]
        offset.append(mlx[s] - mean)
        scale.append(lax.rsqrt(square / n1 + 1e-05) * gains[0:8, :])
        shift.append(gains[8:16, :])
    where = [(0, 0), (0, 1), (0, 2), (1, 0), (1, 1), (1, 2), (1, 3), (1, 4), (1, 5), (0, 3), (0, 4), (0, 5)]
    for g, (s, r) in enumerate(where):
        zed = (dbuf[g].astype(F32) + offset[s][r : r + 1, :]) * scale[s][r : r + 1, :] + shift[s][r : r + 1, :]
        act[:, 128 * g : 128 * (g + 1)] = (zed * jax.nn.sigmoid(zed)).astype(BF16)

    for i in range(3, WCH):
        forward_again(i)
    loads[7].wait()
    arrived(w_rows(sib), "w_sib")
    arrived(w_rows(par_t + 1 - 2 * c), "w_fp")
    for i in range(WCH):
        arrived(w_rows(ext_s, WROWS * i, WROWS), f"w_fe{i}")
    for i in range(WCH):
        arrived(w_rows(pe_t + 1 - 2 * c, WROWS * i, WROWS), f"w_fep{i}")

    def columns(i, _):
        at = pl.multiple_of(256 * i, 256)
        branch = lax.dot_general(
            act[...], wf[pl.ds(at, 256), :], (((1,), (1,)), ((), ())), preferred_element_type=F32
        )
        out[0, :, pl.ds(at, 256)] = (xin[:, pl.ds(at, 256)].astype(F32) + branch).astype(BF16)
        return 0

    lax.fori_loop(0, D // 256, columns, 0)

    for copy in glu_x + [glu_sib] + packs + [w_sib, w_par, w_fp] + glu_f + w_e + w_fwd:
        copy.wait_send()
    for core in range(2):
        pl.when(c == core)(to_partner[core].wait_send)
        pl.when((c == core) & jnp.logical_not(mine))(to_sibling[core].wait_send)
    for cond, copy in halos + given + means:
        pl.when(cond)(copy.wait_send)

    def sent_plane(i, _):
        plane_copy(i).wait_send()
        return 0

    def sent_line(i, _):
        line(i, bmsg, ball, bsend, brecv).wait_send()
        line(i, gmsg, gall, gsend, grecv).wait_send()
        return 0

    lax.fori_loop(1, 32, sent_plane, 0)
    lax.fori_loop(1, 16, sent_line, 0)


def per_device(
    frames_in, lengths, ln_gain, ln_bias, glu_weight, conv_kernel, bn_gain, bn_bias, out_weight
):
    hbm = pl.BlockSpec(memory_space=pl.ANY)
    dma = pltpu.SemaphoreType.DMA
    return pl.pallas_call(
        body,
        out_shape=jax.ShapeDtypeStruct((1, ROWS, D), BF16),
        in_specs=[hbm, pl.BlockSpec(memory_space=pltpu.SMEM)] + [hbm] * 7,
        out_specs=pl.BlockSpec(memory_space=pltpu.VMEM),
        scratch_shapes=[
            pltpu.VMEM((ROWS, D), BF16),
            pltpu.VMEM((1, D), F32),
            pltpu.VMEM((1, D), F32),
            pltpu.VMEM((TAPS, SHARD), BF16),
            pltpu.VMEM((1, SHARD), F32),
            pltpu.VMEM((1, SHARD), F32),
            pltpu.VMEM((ROWS, D), BF16),
            pltpu.VMEM((WIN, D), BF16),
            pltpu.VMEM((2, 2, CHIP, D), BF16),
            pltpu.VMEM((D, D), BF16),
            pltpu.VMEM((4, 40, 256), F32),
            pltpu.VMEM((6, 40, 128), F32),
            pltpu.VMEM((WIN, 128), F32),
            pltpu.VMEM((SPAN, 128), F32),
            pltpu.VMEM((6, SPAN, 128), BF16),
            pltpu.VMEM((12, ROWS, 128), BF16),
            pltpu.VMEM((16, 128), F32),
            pltpu.VMEM((32, 16, 128), F32),
            pltpu.VMEM((16, 128), F32),
            pltpu.VMEM((16, 128), F32),
            pltpu.VMEM((16, 16, 128), F32),
            pltpu.VMEM((16, 16, 128), F32),
            pltpu.VMEM((2, 8, 128), F32),
            pltpu.VMEM((ROWS, D), BF16),
            dma((9,)),
            dma((len(SENDS),)),
            dma((len(NAMES),)),
            dma((32,)),
            dma((32,)),
            dma((16,)),
            dma((16,)),
            dma((16,)),
            dma((16,)),
        ],
        compiler_params=pltpu.CompilerParams(
            collective_id=0, has_side_effects=True, vmem_limit_bytes=48 << 20
        ),
    )(
        frames_in, lengths, ln_gain.reshape(1, D), ln_bias.reshape(1, D), glu_weight, conv_kernel,
        bn_gain.reshape(1, SHARD), bn_bias.reshape(1, SHARD), out_weight,
    )


def solution(mesh):
    return jax.shard_map(
        per_device,
        mesh=mesh,
        in_specs=(
            P("dp", "tensor", None),
            P("dp"),
            P(),
            P(),
            P(None, "tensor", None),
            P(None, "tensor"),
            P("tensor"),
            P("tensor"),
            P("tensor", None),
        ),
        out_specs=P("dp", "tensor", None),
        check_vma=False,
    )
```

time: 589 us -> 100 us (0.17)
  blocking collectives: 409 us -> 0 us
  waiting for transfers between devices: 142 us -> 0 us
  Pallas kernels: 0 us -> 91.7 us
  between operations: 14.2 us -> 0.67 us
  other arithmetic: 12.7 us -> 0 us
  matrix products: 6.12 us -> 0 us
    psum x2 -> x0, blocking collectives: 384 us -> none  [the longest x1 197 us: batch_stats(): sums, count = lax.psum((local_sums, own_count), 'dp')]
    all_gather x2 -> x0, waiting for transfers between devices: 142 us -> none  [the longest x1 89.8 us: per_device(): lax.all_gather(act, 'tensor', axis=1, tiled=True)]
    pallas_call x0 -> x1, Pallas kernels: none -> 91.7 us  [per_device(): pl.pallas_call(body, out_shape=jax.ShapeDtypeStruct((1, ROWS, D), BF16),...]
    all_to_all x1 -> x0, blocking collectives: 25.2 us -> none  [per_device(): lax.all_to_all(partial_cols, 'tensor', split_axis=0, concat_axis=1, tiled...]
    reduce_sum x4 -> x0, other arithmetic: 8.03 us -> none  [the longest x1 7.34 us: batch_stats(): local_sums = reduce_fn(jnp.sum(conv * weight_rows, axis=0)[None])[0]]
    dot_general x2 -> x0, matrix products: 6.12 us -> none  [contract_last(): lax.dot_general(left, right, (((1,), (1,)), ((), ())), preferred_element_...]
  transfers between devices with their start and end apart: 2 -> 0, of which waited for: 2 -> 0; matrix products, arithmetic and copies ran while one was open for 0% -> 0% of each run, Pallas kernels for 0% -> 0%
where the time goes in v1:
time: 100 us; the launch traced here: 99.9 us
  Pallas kernels  91.7 us (92%)
  local copies, waits for them, and re-layouts  7.55 us (8%)
    pallas_call x1, Pallas kernels, per_device(): pl.pallas_call(body, out_shape=jax.ShapeDtypeStruct((1, ROWS, D), BF16),...  91.7 us
    unnamed x13, local copies, waits for them, and re-layouts  6.15 us

profile of v1, /device:TPU:1, one launch (start us, length us, event | category | flops | bytes accessed | tf_op | source)
XLA Modules:
  0.0 99.9 jit_solution(18370029436742380187)
XLA Ops:
  0.7 0.7 reshape.12.ln_gain
  1.4 0.7 reshape.13.ln_bias
  2.1 0.0 copy-start
  2.1 1.3 %copy-done = bf16[2,192,1536]{2,1,0:T(8,128)(2,1)S(1)} copy-done((bf16[2,192,1536]{2,1,0:T(8,128)(2,1)S(1)}, bf16[2,192,1536]{2,1,0:T(8,128)(2,1)}, u32[]{:S(2)}) %copy-start) | copy-done | bytes 1179672
  3.3 0.0 copy-start.1
  3.3 1.1 %copy-done.1 = bf16[192,1536]{1,0:T(8,128)(2,1)S(1)} copy-done((bf16[192,1536]{1,0:T(8,128)(2,1)S(1)}, bf16[192,1536]{1,0:T(8,128)(2,1)}, u32[]{:S(2)}) %copy-start.1) | copy-done | bytes 589848
  4.4 0.0 copy-start.2
  4.4 1.0 copy-done.2
  5.4 0.0 copy-start.3
  5.4 0.7 copy-done.3
  6.1 0.0 copy-start.4
  6.1 0.7 copy-done.4
  6.8 0.0 copy-start.5
  6.8 0.7 copy-done.5
  7.5 91.7 %shard_map.91 = bf16[1,128,1536]{2,1,0:T(8,128)(2,1)S(1)} custom-call(bf16[1,128,1536]{2,1,0:T(8,128)(2,1)S(1)} %copy-done.2, s32[1]{0:T(128)S(6)} %copy.11.lengths, f32[1,1536]{1,0:T(1,128)S(1)} %reshape.12.ln_gain, f32[1,1536]{1,0:T(1,128)S(1)} %reshape.13.ln_bias, bf16[2,192,1536]{2,1,0:T(8,128)(2,1)S(1)} %copy-done, bf16[32,192]{1,0:T(8,128)(2,1)S(1)} %copy-done.3, ...), custom_call_target="tpu_custom_call" | custom-call | tf_op jit(solution)/shard_map/pallas_call | solution.py:521
  99.2 0.7 copy.12
Async XLA Ops:
  2.1 1.3 %copy-start = (bf16[2,192,1536]{2,1,0:T(8,128)(2,1)S(1)}, bf16[2,192,1536]{2,1,0:T(8,128)(2,1)}, u32[]{:S(2)}) copy-start(bf16[2,192,1536]{2,1,0:T(8,128)(2,1)} %glu_w.1) | copy-start | bytes 3538948
  3.3 1.1 %copy-start.1 = (bf16[192,1536]{1,0:T(8,128)(2,1)S(1)}, bf16[192,1536]{1,0:T(8,128)(2,1)}, u32[]{:S(2)}) copy-start(bf16[192,1536]{1,0:T(8,128)(2,1)} %out_w.1) | copy-start | bytes 1769476
  4.4 1.0 copy-start.2
  5.4 0.7 copy-start.3
  6.1 0.7 copy-start.4
  6.8 0.7 copy-start.5

commit v2 on v1

v2 whole, which is shorter than its diff:
```python
import functools

import jax
import jax.numpy as jnp
from jax import lax
from jax.experimental import pallas as pl
from jax.experimental.pallas import tpu as pltpu
from jax.sharding import PartitionSpec as P

MESH = pl.DeviceIdType.MESH
F32 = jnp.float32
BF16 = jnp.bfloat16
TAPS = 32
D = 1536
SHARD = 192
CHIP = 384
ROWS = 128
HALO = 16
SPAN = 2 * ROWS
WIN = SPAN + 2 * HALO
QUARTER = SHARD // 4
CHUNKS = 3
CROWS = QUARTER // CHUNKS
SENDS = 128

NAMES = (
    ["glu_sib", "blk0", "blk1", "low", "high", "pack_s", "pack_e", "pack_d", "w_sib"]
    + [f"gy{i}" for i in range(CHUNKS)]
    + [f"gx{k}_{i}" for k in range(3) for i in range(CHUNKS)]
    + [f"gf{k}_{i}" for k in range(4) for i in range(CHUNKS)]
    + ["we", "wp", "wq"]
    + [f"w{s}x{k}" for s in "epq" for k in range(3)]
    + [f"w{s}f{k}" for s in "epq" for k in range(4)]
    + [f"d{k}_{g}" for k in range(3) for g in range(2)]
    + ["ml0", "ml1"]
    + ["gain0", "gain1"]
)
SEM = {name: i for i, name in enumerate(NAMES)}


def body(
    frames, lengths, ln_gain, ln_bias, glu_w, taps_in, bn_gain, bn_bias, out_w, out,
    xin, lng, lnb, tin, bg, bb, own, nbuf, wg, wf, pack, par, gs, cv, dsend, dbuf,
    msg, plane, bmsg, gmsg, ball, gall, mlx, act,
    lsem, ssem, rsem, asend, arecv, bsend, brecv,
):
    dp = lax.axis_index("dp")
    t = lax.axis_index("tensor")
    x, yh, z = dp // 16, (dp // 8) % 2, dp % 8
    y, c = t // 2, t % 2
    h, j = y // 2, y % 2
    me = yh * 8 + t
    sib = t + 1 - 2 * c
    par_t = (y + 1 - 2 * j) * 2 + c
    ext_t = (3 - y) * 2 + c
    ext_s = (3 - y) * 2 + 1 - c
    edge = (y == 0) | (y == 3)
    ext_dp = jnp.where(edge, dp + 8 - 16 * yh, dp)
    pe_t = (3 - (y + 1 - 2 * j)) * 2 + c

    colour = (x + 2 * z) % 4
    near = [
        ((((x + 1) % 4) * 2 + yh) * 8 + z, (colour + 1) % 4, 1),
        ((((x + 3) % 4) * 2 + yh) * 8 + z, (colour + 3) % 4, 0),
        ((x * 2 + yh) * 8 + z + 1 - 2 * (z % 2), (colour + 2) % 4, 2),
    ]
    sent = []

    def send(src, dst, recv, tensor, to_dp=dp, cond=None):
        copy = pltpu.make_async_remote_copy(
            src_ref=src, dst_ref=dst, send_sem=ssem.at[len(sent)], recv_sem=rsem.at[SEM[recv]],
            device_id={"dp": to_dp, "tensor": tensor}, device_id_type=MESH,
        )
        sent.append((cond, copy))
        if cond is None:
            copy.start()
        else:
            pl.when(cond)(copy.start)

    def arrived(dst, recv):
        pltpu.make_async_remote_copy(
            src_ref=dst, dst_ref=dst, send_sem=ssem.at[0], recv_sem=rsem.at[SEM[recv]],
            device_id={"dp": dp, "tensor": sib}, device_id_type=MESH,
        ).wait_recv()

    barrier = pltpu.get_barrier_semaphore()

    def greet_plane(i, _):
        to = (((x + i // 8) % 4) * 2 + yh) * 8 + (z + i % 8) % 8
        pl.semaphore_signal(barrier, inc=1, device_id={"dp": to, "tensor": t}, device_id_type=MESH)
        return 0

    def greet_line(i, _):
        q = (me + i) % 16
        to = (x * 2 + q // 8) * 8 + z
        pl.semaphore_signal(barrier, inc=1, device_id={"dp": to, "tensor": q % 8}, device_id_type=MESH)
        return 0

    lax.fori_loop(1, 16, greet_line, 0)
    lax.fori_loop(1, 32, greet_plane, 0)

    loads = [
        pltpu.make_async_copy(frames.at[0], xin, lsem.at[0]),
        pltpu.make_async_copy(ln_gain, lng, lsem.at[1]),
        pltpu.make_async_copy(ln_bias, lnb, lsem.at[2]),
        pltpu.make_async_copy(taps_in, tin, lsem.at[3]),
        pltpu.make_async_copy(bn_gain, bg, lsem.at[4]),
        pltpu.make_async_copy(bn_bias, bb, lsem.at[5]),
        pltpu.make_async_copy(glu_w, wg.at[h, :, pl.ds(pl.multiple_of(SHARD * c, 64), SHARD)], lsem.at[6]),
        pltpu.make_async_copy(out_w, wf.at[pl.ds(pl.multiple_of(SHARD * t, 64), SHARD)], lsem.at[7]),
    ]
    for copy in loads:
        copy.start()
    for copy in loads[:6]:
        copy.wait()

    rows = xin[...].astype(F32)
    center = jnp.mean(rows, axis=-1, keepdims=True)
    spread = jnp.mean((rows - center) ** 2, axis=-1, keepdims=True)
    own[...] = ((rows - center) * lax.rsqrt(spread + 1e-05) * lng[...][None, :] + lnb[...][None, :]).astype(BF16)

    pack[0] = jnp.zeros_like(pack[0])
    pack[0, 0:TAPS, 0:SHARD] = tin[...].astype(F32)
    pack[0, TAPS : TAPS + 1, 0:SHARD] = bg[...][None, :]
    pack[0, TAPS + 1 : TAPS + 2, 0:SHARD] = bb[...][None, :]

    same = (y + 2 * c - 1) // 2 == h
    gives = ((c == 1) & (y < 3)) | ((c == 0) & (y > 0))
    y2 = y + 2 * c - 1
    h2, j2 = y2 // 2, (y2 + 2) % 2
    mine = j == c

    @pl.when(mine)
    def _():
        nbuf[pl.ds(pl.multiple_of(HALO + ROWS * c, 16), ROWS), :] = own[...]

    @pl.when((c == 1) & (j == 0))
    def _():
        nbuf[0:HALO, :] = own[ROWS - HALO : ROWS, :]

    @pl.when((c == 0) & (j == 1))
    def _():
        nbuf[WIN - HALO : WIN, :] = own[0:HALO, :]

    @pl.when((c == 0) & (h == 0))
    def _():
        nbuf[0:HALO, :] = jnp.zeros((HALO, D), BF16)

    @pl.when((c == 1) & (h == 1))
    def _():
        nbuf[WIN - HALO : WIN, :] = jnp.zeros((HALO, D), BF16)

    pl.semaphore_wait(barrier, 46)

    def glu_rows(slot, core, quarter, i):
        first = SHARD * core + QUARTER * quarter + CROWS * i
        return wg.at[slot, :, pl.ds(pl.multiple_of(first, 16), CROWS)]

    for i in range(CHUNKS):
        src = glu_w.at[:, pl.ds(pl.multiple_of(QUARTER * colour + CROWS * i, 16), CROWS)]
        send(src, glu_rows(h, c, colour, i), f"gy{i}", ext_t, ext_dp)

    away = jnp.logical_not(mine)
    spot = nbuf.at[pl.ds(pl.multiple_of(HALO + ROWS * c, 16), ROWS)]
    for core in range(2):
        send(own, spot, f"blk{core}", (y + 1 - 2 * j) * 2 + j, cond=c == core)
        send(own, spot, f"blk{core}", sib, cond=(c == core) & away)

    low = nbuf.at[0:HALO]
    high = nbuf.at[WIN - HALO : WIN]
    tail = own.at[ROWS - HALO : ROWS]
    head = own.at[0:HALO]
    halo_a = jnp.where(same, par_t, (2 * h2) * 2 + j2)
    halo_b = (2 * h2 + 1) * 2 + j2
    apart = jnp.logical_not(same)
    send(tail, low, "low", halo_a, cond=(c == 1) & gives)
    send(tail, low, "low", halo_b, cond=(c == 1) & gives & apart)
    send(head, high, "high", halo_a, cond=(c == 0) & gives)
    send(head, high, "high", halo_b, cond=(c == 0) & gives & apart)

    send(glu_w, wg.at[h, :, pl.ds(pl.multiple_of(SHARD * c, 64), SHARD)], "glu_sib", sib)
    send(pack.at[0], pack.at[1], "pack_s", sib)
    send(pack.at[0], pack.at[2], "pack_e", ext_t, ext_dp)
    send(pack.at[0], pack.at[3], "pack_d", ext_s, ext_dp)

    def w_rows(shard, first=0, n=SHARD):
        return wf.at[pl.ds(pl.multiple_of(SHARD * shard + first, 16), n)]

    def w_quarter(shard, quarter):
        return w_rows(shard, QUARTER * quarter, QUARTER)

    send(out_w, w_rows(t), "w_sib", sib)

    lane = lax.broadcasted_iota(jnp.int32, (40, 128), 1)

    def tiles_of(slot, mine_at, other_at):
        a = pack[mine_at]
        b = pack[other_at]
        first = jnp.where(c == 0, a, b)
        second = jnp.where(c == 0, b, a)
        r0 = pltpu.roll(second[:, 0:128], 64, 1)
        r1 = pltpu.roll(second[:, 128:256], 64, 1)
        par[3 * slot] = first[:, 0:128]
        par[3 * slot + 1] = jnp.where(lane < 64, first[:, 128:256], r0)
        par[3 * slot + 2] = jnp.where(lane < 64, r0, r1)

    arrived(pack.at[1], "pack_s")
    tiles_of(h, 0, 1)
    arrived(pack.at[2], "pack_e")
    arrived(pack.at[3], "pack_d")
    tiles_of(1 - h, 2, 3)
    gmsg[...] = jnp.zeros_like(gmsg)
    for k in range(6):
        gmsg[k : k + 1, :] = par[k, TAPS : TAPS + 1, :]
        gmsg[8 + k : 9 + k, :] = par[k, TAPS + 1 : TAPS + 2, :]

    for giver in range(2):
        is_giver = t == 2 * giver
        for i in range(1, 8):
            send(gmsg, gall.at[giver], f"gain{giver}", (t + i) % 8, cond=is_giver)

        @pl.when(is_giver)
        def _(giver=giver):
            gall[giver] = gmsg[...]

    length = lengths[0]
    start = 2 * SPAN * h + SPAN * c
    count = jnp.clip(length - start, 0, SPAN)
    count_f = count.astype(F32)
    inverse = 1.0 / jnp.maximum(count_f, 1.0)
    msg[...] = jnp.zeros_like(msg)
    msg[6:7, :] = jnp.full((1, 128), count_f, F32)

    def one_tile(slot, q):
        k = 3 * slot + q
        w = wg[slot, :, pl.ds(pl.multiple_of(128 * q, 128), 128), :].reshape(256, D)
        both = lax.dot_general(nbuf[...], w, (((1,), (1,)), ((), ())), preferred_element_type=F32)
        glu = (both[:, 0:128] * jax.nn.sigmoid(both[:, 128:256])).astype(BF16).astype(F32)
        at = lax.broadcasted_iota(jnp.int32, (WIN, 128), 0)
        gs[...] = jnp.where(at < length - start + HALO, glu, 0.0)
        step = 64

        def conv_rows(i, total):
            first = pl.multiple_of(i * step, step)
            acc = jnp.zeros((step, 128), F32)
            for tap in range(TAPS):
                acc = acc + gs[pl.ds(first + (tap + 1), step), :] * par[k, tap : tap + 1, :]
            cv[pl.ds(first, step), :] = acc
            here = first + lax.broadcasted_iota(jnp.int32, (step, 128), 0)
            kept = jnp.where(here < count, acc, 0.0)
            return total + jnp.sum(kept.reshape(step // 8, 8, 128), axis=0)

        total = lax.fori_loop(0, SPAN // step, conv_rows, jnp.zeros((8, 128), F32))
        local = jnp.sum(total, axis=0, keepdims=True) * inverse
        dev = cv[...] - local
        dsend[k] = dev.astype(BF16)
        here = lax.broadcasted_iota(jnp.int32, (SPAN, 128), 0)
        kept = jnp.where(here < count, dev, 0.0)
        msg[pl.ds(k, 1), :] = local
        msg[pl.ds(8 + k, 1), :] = jnp.sum(kept * kept, axis=0, keepdims=True)

    owner = 2 * (2 * h + c)
    shard_of = (jnp.minimum(y, 3 - y), jnp.maximum(y, 3 - y))

    def give(slot, q, n, group):
        base = 3 * jnp.where(slot == 0, shard_of[0], shard_of[1]) + q
        for g in range(2):
            src = dsend.at[pl.ds(3 * slot + q, n), pl.ds(ROWS * g, ROWS)]
            dst = dbuf.at[pl.ds(base, n)]
            kept = mine & (c == g)
            for s in range(2):
                send(src, dst, f"d{group}_{s}", owner + g, cond=jnp.logical_not(kept) & (j == s))

            @pl.when(kept)
            def _(src=src, dst=dst):
                keep = pltpu.make_async_copy(src, dst, lsem.at[8])
                keep.start()
                keep.wait()

    for i in range(CHUNKS):
        at = glu_rows(1 - h, c, colour, i)
        arrived(at, f"gy{i}")
        for to_dp, _, k in near:
            send(at, at, f"gx{k}_{i}", t, to_dp)
        send(at, at, f"gf3_{i}", sib)

    def pass_glu(i):
        for k, (_, their, _) in enumerate(near):
            at = glu_rows(1 - h, c, their, i)
            arrived(at, f"gx{k}_{i}")
            send(at, at, f"gf{k}_{i}", sib)

    for p in range(2):
        @pl.when(jnp.logical_not(mine & (c == p)))
        def _(p=p):
            arrived(nbuf.at[HALO + ROWS * p : HALO + ROWS * (p + 1)], f"blk{p}")

    @pl.when(((c == 1) & (j == 1)) | ((c == 0) & (h == 1)))
    def _():
        arrived(low, "low")

    @pl.when(((c == 0) & (j == 0)) | ((c == 1) & (h == 0)))
    def _():
        arrived(high, "high")

    loads[6].wait()
    arrived(wg.at[h, :, pl.ds(pl.multiple_of(SHARD * (1 - c), 64), SHARD)], "glu_sib")

    w_mine = out_w.at[pl.ds(pl.multiple_of(QUARTER * colour, 16), QUARTER)]
    send(w_mine, w_quarter(t, colour), "we", ext_t, ext_dp)
    send(w_mine, w_quarter(t, colour), "wp", par_t)

    one_tile(h, 0)
    pass_glu(0)
    one_tile(h, 1)
    pass_glu(1)
    one_tile(h, 2)
    pass_glu(2)
    give(h, 0, 3, 0)

    w_from = {"e": ext_t, "p": par_t, "q": pe_t}

    def w_on(s):
        at = w_quarter(w_from[s], colour)
        arrived(at, f"w{s}")
        if s == "e":
            send(at, at, "wq", par_t)
        for to_dp, _, k in near:
            send(at, at, f"w{s}x{k}", t, to_dp)
        send(at, at, f"w{s}f3", sib)

    def w_last(s):
        for k, (_, their, _) in enumerate(near):
            at = w_quarter(w_from[s], their)
            arrived(at, f"w{s}x{k}")
            send(at, at, f"w{s}f{k}", sib)

    quarters = [their for _, their, _ in near] + [colour]
    for i in range(CHUNKS):
        for k in range(4):
            arrived(glu_rows(1 - h, 1 - c, quarters[k], i), f"gf{k}_{i}")
    one_tile(1 - h, 0)
    w_on("e")
    w_on("p")
    one_tile(1 - h, 1)
    give(1 - h, 0, 1, 1)
    one_tile(1 - h, 2)

    def plane_copy(i):
        to = (((x + i // 8) % 4) * 2 + yh) * 8 + (z + i % 8) % 8
        return pltpu.make_async_remote_copy(
            src_ref=msg, dst_ref=plane.at[i], send_sem=asend.at[i], recv_sem=arecv.at[i],
            device_id={"dp": to, "tensor": t}, device_id_type=MESH,
        )

    def send_plane(i, _):
        plane_copy(i).start()
        return 0

    lax.fori_loop(1, 32, send_plane, 0)
    give(1 - h, 1, 2, 2)
    u = jnp.where(edge, 0, 1)
    for g in range(2):
        for s in range(2):
            send(msg.at[0:8], mlx.at[s], f"ml{s}", owner + g, cond=jnp.logical_not(mine & (c == g)) & (u == s))

    @pl.when(mine)
    def _():
        mlx[u] = msg[0:8, :]

    w_on("q")

    def merge(blocks):
        n = sum(jnp.broadcast_to(b[6:7, :], (8, 128)) for b in blocks)
        weighted = sum(jnp.broadcast_to(b[6:7, :], (8, 128)) * b[0:8, :] for b in blocks)
        mean = weighted / jnp.maximum(n, 1.0)
        square = sum(
            b[8:16, :] + jnp.broadcast_to(b[6:7, :], (8, 128)) * (b[0:8, :] - mean) ** 2 for b in blocks
        )
        return n, mean, square

    def wait_plane(i, _):
        plane_copy(i).wait_recv()
        return 0

    lax.fori_loop(1, 32, wait_plane, 0)
    plane[0] = msg[...]
    n, mean, square = merge([plane[i] for i in range(32)])
    row = lax.broadcasted_iota(jnp.int32, (8, 128), 0)
    bmsg[0:8, :] = jnp.where(row == 6, n, mean)
    bmsg[8:16, :] = square

    def line(i, src, dst, ss, rs):
        q = (me + i) % 16
        to = (x * 2 + q // 8) * 8 + z
        return pltpu.make_async_remote_copy(
            src_ref=src, dst_ref=dst.at[me], send_sem=ss.at[i], recv_sem=rs.at[me],
            device_id={"dp": to, "tensor": q % 8}, device_id_type=MESH,
        )

    def send_line(i, _):
        line(i, bmsg, ball, bsend, brecv).start()
        return 0

    lax.fori_loop(1, 16, send_line, 0)
    ball[me] = bmsg[...]

    for s in "epq":
        w_last(s)

    def wait_line(i, _):
        q = (me + i) % 16
        pltpu.make_async_remote_copy(
            src_ref=bmsg, dst_ref=ball.at[q], send_sem=bsend.at[0], recv_sem=brecv.at[q],
            device_id={"dp": dp, "tensor": sib}, device_id_type=MESH,
        ).wait_recv()
        return 0

    lax.fori_loop(1, 16, wait_line, 0)

    for group, n in ((0, 3), (1, 1), (2, 2)):
        for s in range(2):
            @pl.when(jnp.logical_not((j == s) & mine))
            def _(group=group, n=n, s=s):
                arrived(dbuf.at[pl.ds(0, n)], f"d{group}_{s}")
    for s in range(2):
        @pl.when(jnp.logical_not((u == s) & mine))
        def _(s=s):
            arrived(mlx.at[s], f"ml{s}")

    for giver in range(2):
        @pl.when(t != 2 * giver)
        def _(giver=giver):
            arrived(gall.at[giver], f"gain{giver}")

    sets = ((0, 1, 6, 7), (2, 3, 4, 5))
    offset, scale, shift = [], [], []
    for s in range(2):
        n, mean, square = merge([ball[8 * g + q] for g in range(2) for q in sets[s]])
        n1 = jnp.broadcast_to(n[0:1, :], (8, 128))
        gains = gall[s]
        offset.append(mlx[s] - mean)
        scale.append(lax.rsqrt(square / n1 + 1e-05) * gains[0:8, :])
        shift.append(gains[8:16, :])
    where = [(0, 0), (0, 1), (0, 2), (1, 0), (1, 1), (1, 2), (1, 3), (1, 4), (1, 5), (0, 3), (0, 4), (0, 5)]
    for g, (s, r) in enumerate(where):
        zed = (dbuf[g].astype(F32) + offset[s][r : r + 1, :]) * scale[s][r : r + 1, :] + shift[s][r : r + 1, :]
        act[:, 128 * g : 128 * (g + 1)] = (zed * jax.nn.sigmoid(zed)).astype(BF16)

    loads[7].wait()
    arrived(w_rows(sib), "w_sib")
    for s in "epq":
        for k in range(4):
            arrived(w_quarter(w_from[s] + 1 - 2 * c, quarters[k]), f"w{s}f{k}")

    def columns(i, _):
        at = pl.multiple_of(256 * i, 256)
        branch = lax.dot_general(
            act[...], wf[pl.ds(at, 256), :], (((1,), (1,)), ((), ())), preferred_element_type=F32
        )
        out[0, :, pl.ds(at, 256)] = (xin[:, pl.ds(at, 256)].astype(F32) + branch).astype(BF16)
        return 0

    lax.fori_loop(0, D // 256, columns, 0)

    for cond, copy in sent:
        if cond is None:
            copy.wait_send()
        else:
            pl.when(cond)(copy.wait_send)

    def sent_plane(i, _):
        plane_copy(i).wait_send()
        return 0

    def sent_line(i, _):
        line(i, bmsg, ball, bsend, brecv).wait_send()
        return 0

    lax.fori_loop(1, 32, sent_plane, 0)
    lax.fori_loop(1, 16, sent_line, 0)


def per_device(
    frames_in, lengths, ln_gain, ln_bias, glu_weight, conv_kernel, bn_gain, bn_bias, out_weight
):
    hbm = pl.BlockSpec(memory_space=pltpu.HBM)
    dma = pltpu.SemaphoreType.DMA
    return pl.pallas_call(
        body,
        out_shape=jax.ShapeDtypeStruct((1, ROWS, D), BF16),
        in_specs=[hbm, pl.BlockSpec(memory_space=pltpu.SMEM)] + [hbm] * 7,
        out_specs=pl.BlockSpec(memory_space=pltpu.VMEM),
        scratch_shapes=[
            pltpu.VMEM((ROWS, D), BF16),
            pltpu.VMEM((D,), F32),
            pltpu.VMEM((D,), F32),
            pltpu.VMEM((TAPS, SHARD), BF16),
            pltpu.VMEM((SHARD,), F32),
            pltpu.VMEM((SHARD,), F32),
            pltpu.VMEM((ROWS, D), BF16),
            pltpu.VMEM((WIN, D), BF16),
            pltpu.VMEM((2, 2, CHIP, D), BF16),
            pltpu.VMEM((D, D), BF16),
            pltpu.VMEM((4, 40, 256), F32),
            pltpu.VMEM((6, 40, 128), F32),
            pltpu.VMEM((WIN, 128), F32),
            pltpu.VMEM((SPAN, 128), F32),
            pltpu.VMEM((6, SPAN, 128), BF16),
            pltpu.VMEM((12, ROWS, 128), BF16),
            pltpu.VMEM((16, 128), F32),
            pltpu.VMEM((32, 16, 128), F32),
            pltpu.VMEM((16, 128), F32),
            pltpu.VMEM((16, 128), F32),
            pltpu.VMEM((16, 16, 128), F32),
            pltpu.VMEM((2, 16, 128), F32),
            pltpu.VMEM((2, 8, 128), F32),
            pltpu.VMEM((ROWS, D), BF16),
            dma((9,)),
            dma((SENDS,)),
            dma((len(NAMES),)),
            dma((32,)),
            dma((32,)),
            dma((16,)),
            dma((16,)),
        ],
        compiler_params=pltpu.CompilerParams(
            collective_id=0, has_side_effects=True, vmem_limit_bytes=(64 << 20) - (128 << 10)
        ),
    )(
        frames_in, lengths, ln_gain, ln_bias, glu_weight, conv_kernel,
        bn_gain, bn_bias, out_weight,
    )


def solution(mesh):
    return jax.shard_map(
        per_device,
        mesh=mesh,
        in_specs=(
            P("dp", "tensor", None),
            P("dp"),
            P(),
            P(),
            P(None, "tensor", None),
            P(None, "tensor"),
            P("tensor"),
            P("tensor"),
            P("tensor", None),
        ),
        out_specs=P("dp", "tensor", None),
        check_vma=False,
    )
```

time: 100 us -> 68.5 us (0.69)
  Pallas kernels: 91.7 us -> 65.9 us
  local copies, waits for them, and re-layouts: 7.55 us -> 1.77 us
    pallas_call x1, Pallas kernels: 91.7 us -> 65.9 us  [per_device(): pl.pallas_call(body, out_shape=jax.ShapeDtypeStruct((1, ROWS, D), BF16),...]
    unnamed x13 -> x1, local copies, waits for them, and re-layouts: 6.15 us -> 1.77 us
    reshape x2 -> x0, local copies, waits for them, and re-layouts: 1.4 us -> none  [the longest x1 0.7 us: per_device(): ln_gain.reshape(1, D)]
where the time goes in v2:
time: 68.5 us; the launch traced here: 68.3 us
  Pallas kernels  65.9 us (96%)
  local copies, waits for them, and re-layouts  1.77 us (3%)
    pallas_call x1, Pallas kernels, per_device(): pl.pallas_call(body, out_shape=jax.ShapeDtypeStruct((1, ROWS, D), BF16),...  65.9 us
    unnamed x1, local copies, waits for them, and re-layouts  1.77 us

profile of v2, /device:TPU:1, one launch (start us, length us, event | category | flops | bytes accessed | tf_op | source)
XLA Modules:
  0.0 68.3 jit_solution(71055835506810553)
XLA Ops:
  0.7 65.9 %shard_map.91 = bf16[1,128,1536]{2,1,0:T(8,128)(2,1)} custom-call(bf16[1,128,1536]{2,1,0:T(8,128)(2,1)} %frames.1, s32[1]{0:T(128)S(6)} %copy.11.lengths, f32[1536]{0:T(1024)} %ln_gain.1, f32[1536]{0:T(1024)} %ln_bias.1, bf16[2,192,1536]{2,1,0:T(8,128)(2,1)} %glu_w.1, bf16[32,192]{1,0:T(8,128)(2,1)} %taps_in.1, f32[192]{0:T(256)} %bn_gain.1, f32[192]{0:T(256)} %bn_bias.1, ...), custom_call_target="tpu_custom_call" | custom-call | tf_op jit(solution)/shard_map/pallas_call | solution.py:489
  66.5 1.8 %copy.12 = bf16[1,128,1536]{2,1,0:T(8,128)(2,1)} copy(bf16[1,128,1536]{2,1,0:T(8,128)(2,1)} %shard_map.91) | data formatting | bytes 786432

commit v3 on v2

v3 whole, which is shorter than its diff:
```python
import functools

import jax
import jax.numpy as jnp
from jax import lax
from jax.experimental import pallas as pl
from jax.experimental.pallas import tpu as pltpu
from jax.sharding import PartitionSpec as P

MESH = pl.DeviceIdType.MESH
F32 = jnp.float32
BF16 = jnp.bfloat16
TAPS = 32
D = 1536
SHARD = 192
CHIP = 384
ROWS = 128
HALO = 16
SPAN = 2 * ROWS
WIN = SPAN + 2 * HALO
QUARTER = SHARD // 4
CHUNKS = 3
CROWS = QUARTER // CHUNKS
LNS = 4
LROWS = ROWS // LNS
SENDS = 160

NAMES = (
    ["glu_sib", "low", "high", "pack_s", "pack_e", "pack_d", "w_sib"]
    + [f"blk{p}_{i}" for p in range(2) for i in range(LNS)]
    + [f"gy{i}" for i in range(CHUNKS)]
    + [f"gx{k}_{i}" for k in range(3) for i in range(CHUNKS)]
    + [f"gf{k}_{i}" for k in range(4) for i in range(CHUNKS)]
    + ["we", "wp", "wq"]
    + [f"w{s}x{k}" for s in "epq" for k in range(3)]
    + [f"w{s}f{k}" for s in "epq" for k in range(4)]
    + [f"d{k}_{g}" for k in range(3) for g in range(2)]
    + ["ml0", "ml1"]
    + ["gain0", "gain1"]
)
SEM = {name: i for i, name in enumerate(NAMES)}


def body(
    frames, lengths, ln_gain, ln_bias, glu_w, taps_in, bn_gain, bn_bias, out_w, out,
    xin, lng, lnb, tin, bg, bb, own, nbuf, wg, wf, pack, par, gs, cv, dsend, dbuf,
    msg, plane, bmsg, gmsg, ball, gall, mlx, mlm, act,
    lsem, ssem, rsem, asend, arecv, bsend, brecv,
):
    dp = lax.axis_index("dp")
    t = lax.axis_index("tensor")
    x, yh, z = dp // 16, (dp // 8) % 2, dp % 8
    y, c = t // 2, t % 2
    h, j = y // 2, y % 2
    me = yh * 8 + t
    sib = t + 1 - 2 * c
    par_t = (y + 1 - 2 * j) * 2 + c
    ext_t = (3 - y) * 2 + c
    ext_s = (3 - y) * 2 + 1 - c
    edge = (y == 0) | (y == 3)
    ext_dp = jnp.where(edge, dp + 8 - 16 * yh, dp)
    pe_t = (3 - (y + 1 - 2 * j)) * 2 + c

    colour = (x + 2 * z) % 4
    near = [
        ((((x + 1) % 4) * 2 + yh) * 8 + z, (colour + 1) % 4, 1),
        ((((x + 3) % 4) * 2 + yh) * 8 + z, (colour + 3) % 4, 0),
        ((x * 2 + yh) * 8 + z + 1 - 2 * (z % 2), (colour + 2) % 4, 2),
    ]
    sent = []

    def send(src, dst, recv, tensor, to_dp=dp, cond=None):
        copy = pltpu.make_async_remote_copy(
            src_ref=src, dst_ref=dst, send_sem=ssem.at[len(sent)], recv_sem=rsem.at[SEM[recv]],
            device_id={"dp": to_dp, "tensor": tensor}, device_id_type=MESH,
        )
        sent.append((cond, copy))
        if cond is None:
            copy.start()
        else:
            pl.when(cond)(copy.start)

    def arrived(dst, recv):
        pltpu.make_async_remote_copy(
            src_ref=dst, dst_ref=dst, send_sem=ssem.at[0], recv_sem=rsem.at[SEM[recv]],
            device_id={"dp": dp, "tensor": sib}, device_id_type=MESH,
        ).wait_recv()

    barrier = pltpu.get_barrier_semaphore()

    loads = [
        pltpu.make_async_copy(frames.at[0], xin, lsem.at[0]),
        pltpu.make_async_copy(ln_gain, lng, lsem.at[1]),
        pltpu.make_async_copy(ln_bias, lnb, lsem.at[2]),
        pltpu.make_async_copy(taps_in, tin, lsem.at[3]),
        pltpu.make_async_copy(bn_gain, bg, lsem.at[4]),
        pltpu.make_async_copy(bn_bias, bb, lsem.at[5]),
        pltpu.make_async_copy(glu_w, wg.at[h, :, pl.ds(pl.multiple_of(SHARD * c, 64), SHARD)], lsem.at[6]),
        pltpu.make_async_copy(out_w, wf.at[pl.ds(pl.multiple_of(SHARD * t, 64), SHARD)], lsem.at[7]),
    ]
    for copy in loads:
        copy.start()

    def greet_plane(i, _):
        to = (((x + i // 8) % 4) * 2 + yh) * 8 + (z + i % 8) % 8
        pl.semaphore_signal(barrier, inc=1, device_id={"dp": to, "tensor": t}, device_id_type=MESH)
        return 0

    def greet_line(i, _):
        q = (me + i) % 16
        to = (x * 2 + q // 8) * 8 + z
        pl.semaphore_signal(barrier, inc=1, device_id={"dp": to, "tensor": q % 8}, device_id_type=MESH)
        return 0

    lax.fori_loop(1, 16, greet_line, 0)
    lax.fori_loop(1, 32, greet_plane, 0)

    pl.semaphore_wait(barrier, 46)

    same = (y + 2 * c - 1) // 2 == h
    gives = ((c == 1) & (y < 3)) | ((c == 0) & (y > 0))
    y2 = y + 2 * c - 1
    h2, j2 = y2 // 2, (y2 + 2) % 2
    mine = j == c

    def glu_rows(slot, core, quarter, i):
        first = SHARD * core + QUARTER * quarter + CROWS * i
        return wg.at[slot, :, pl.ds(pl.multiple_of(first, 16), CROWS)]

    def w_rows(shard, first=0, n=SHARD):
        return wf.at[pl.ds(pl.multiple_of(SHARD * shard + first, 16), n)]

    def w_quarter(shard, quarter):
        return w_rows(shard, QUARTER * quarter, QUARTER)

    for i in range(CHUNKS):
        src = glu_w.at[:, pl.ds(pl.multiple_of(QUARTER * colour + CROWS * i, 16), CROWS)]
        send(src, glu_rows(h, c, colour, i), f"gy{i}", ext_t, ext_dp)
    send(glu_w, wg.at[h, :, pl.ds(pl.multiple_of(SHARD * c, 64), SHARD)], "glu_sib", sib)

    for copy in loads[:3]:
        copy.wait()
    away = jnp.logical_not(mine)
    for i in range(LNS):
        at = slice(LROWS * i, LROWS * (i + 1))
        rows = xin[at, :].astype(F32)
        center = jnp.mean(rows, axis=-1, keepdims=True)
        spread = jnp.mean((rows - center) ** 2, axis=-1, keepdims=True)
        own[at, :] = (
            (rows - center) * lax.rsqrt(spread + 1e-05) * lng[...][None, :] + lnb[...][None, :]
        ).astype(BF16)
        spot = nbuf.at[pl.ds(pl.multiple_of(HALO + ROWS * c + LROWS * i, 16), LROWS)]
        for core in range(2):
            send(own.at[at], spot, f"blk{core}_{i}", (y + 1 - 2 * j) * 2 + j, cond=c == core)
            send(own.at[at], spot, f"blk{core}_{i}", sib, cond=(c == core) & away)

    low = nbuf.at[0:HALO]
    high = nbuf.at[WIN - HALO : WIN]
    tail = own.at[ROWS - HALO : ROWS]
    head = own.at[0:HALO]
    halo_a = jnp.where(same, par_t, (2 * h2) * 2 + j2)
    halo_b = (2 * h2 + 1) * 2 + j2
    apart = jnp.logical_not(same)
    send(tail, low, "low", halo_a, cond=(c == 1) & gives)
    send(tail, low, "low", halo_b, cond=(c == 1) & gives & apart)
    send(head, high, "high", halo_a, cond=(c == 0) & gives)
    send(head, high, "high", halo_b, cond=(c == 0) & gives & apart)

    for copy in loads[3:6]:
        copy.wait()
    pack[0] = jnp.zeros_like(pack[0])
    pack[0, 0:TAPS, 0:SHARD] = tin[...].astype(F32)
    pack[0, TAPS : TAPS + 1, 0:SHARD] = bg[...][None, :]
    pack[0, TAPS + 1 : TAPS + 2, 0:SHARD] = bb[...][None, :]
    send(pack.at[0], pack.at[1], "pack_s", sib)
    send(pack.at[0], pack.at[2], "pack_e", ext_t, ext_dp)

    @pl.when(mine)
    def _():
        nbuf[pl.ds(pl.multiple_of(HALO + ROWS * c, 16), ROWS), :] = own[...]

    @pl.when((c == 1) & (j == 0))
    def _():
        nbuf[0:HALO, :] = own[ROWS - HALO : ROWS, :]

    @pl.when((c == 0) & (j == 1))
    def _():
        nbuf[WIN - HALO : WIN, :] = own[0:HALO, :]

    @pl.when((c == 0) & (h == 0))
    def _():
        nbuf[0:HALO, :] = jnp.zeros((HALO, D), BF16)

    @pl.when((c == 1) & (h == 1))
    def _():
        nbuf[WIN - HALO : WIN, :] = jnp.zeros((HALO, D), BF16)

    lane = lax.broadcasted_iota(jnp.int32, (40, 128), 1)

    def tiles_of(slot, mine_at, other_at):
        a = pack[mine_at]
        b = pack[other_at]
        first = jnp.where(c == 0, a, b)
        second = jnp.where(c == 0, b, a)
        r0 = pltpu.roll(second[:, 0:128], 64, 1)
        r1 = pltpu.roll(second[:, 128:256], 64, 1)
        par[3 * slot] = first[:, 0:128]
        par[3 * slot + 1] = jnp.where(lane < 64, first[:, 128:256], r0)
        par[3 * slot + 2] = jnp.where(lane < 64, r0, r1)

    arrived(pack.at[1], "pack_s")
    tiles_of(h, 0, 1)
    length = lengths[0]
    start = 2 * SPAN * h + SPAN * c
    count = jnp.clip(length - start, 0, SPAN)
    count_f = count.astype(F32)
    inverse = 1.0 / jnp.maximum(count_f, 1.0)
    msg[...] = jnp.zeros_like(msg)
    mlm[...] = jnp.zeros_like(mlm)
    for kind in range(2):
        msg[kind, 6:7, :] = jnp.full((1, 128), count_f, F32)

    def one_tile(slot, q, kind):
        k = 3 * slot + q
        w = wg[slot, :, pl.ds(pl.multiple_of(128 * q, 128), 128), :].reshape(256, D)
        both = lax.dot_general(nbuf[...], w, (((1,), (1,)), ((), ())), preferred_element_type=F32)
        glu = (both[:, 0:128] * jax.nn.sigmoid(both[:, 128:256])).astype(BF16).astype(F32)
        at = lax.broadcasted_iota(jnp.int32, (WIN, 128), 0)
        gs[...] = jnp.where(at < length - start + HALO, glu, 0.0)
        step = 64

        def conv_rows(i, total):
            first = pl.multiple_of(i * step, step)
            acc = jnp.zeros((step, 128), F32)
            for tap in range(TAPS):
                acc = acc + gs[pl.ds(first + (tap + 1), step), :] * par[k, tap : tap + 1, :]
            cv[pl.ds(first, step), :] = acc
            here = first + lax.broadcasted_iota(jnp.int32, (step, 128), 0)
            kept = jnp.where(here < count, acc, 0.0)
            return total + jnp.sum(kept.reshape(step // 8, 8, 128), axis=0)

        total = lax.fori_loop(0, SPAN // step, conv_rows, jnp.zeros((8, 128), F32))
        local = jnp.sum(total, axis=0, keepdims=True) * inverse
        dev = cv[...] - local
        dsend[k] = dev.astype(BF16)
        here = lax.broadcasted_iota(jnp.int32, (SPAN, 128), 0)
        kept = jnp.where(here < count, dev, 0.0)
        mlm[pl.ds(k, 1), :] = local
        msg[kind, q : q + 1, :] = local
        msg[kind, 3 + q : 4 + q, :] = jnp.sum(kept * kept, axis=0, keepdims=True)

    owner = 2 * (2 * h + c)
    shard_of = (jnp.minimum(y, 3 - y), jnp.maximum(y, 3 - y))

    def give(slot, q, n, group):
        base = 3 * jnp.where(slot == 0, shard_of[0], shard_of[1]) + q
        for g in range(2):
            src = dsend.at[pl.ds(3 * slot + q, n), pl.ds(ROWS * g, ROWS)]
            dst = dbuf.at[pl.ds(base, n)]
            kept = mine & (c == g)
            for s in range(2):
                send(src, dst, f"d{group}_{s}", owner + g, cond=jnp.logical_not(kept) & (j == s))

            @pl.when(kept)
            def _(src=src, dst=dst):
                keep = pltpu.make_async_copy(src, dst, lsem.at[8])
                keep.start()
                keep.wait()

    w_mine = out_w.at[pl.ds(pl.multiple_of(QUARTER * colour, 16), QUARTER)]
    for i in range(CHUNKS):
        at = glu_rows(1 - h, c, colour, i)
        arrived(at, f"gy{i}")
        for to_dp, _, k in near:
            send(at, at, f"gx{k}_{i}", t, to_dp)
        send(at, at, f"gf3_{i}", sib)
        if i == 1:
            send(w_mine, w_quarter(t, colour), "we", ext_t, ext_dp)

    def pass_glu(i):
        for k, (_, their, _) in enumerate(near):
            at = glu_rows(1 - h, c, their, i)
            arrived(at, f"gx{k}_{i}")
            send(at, at, f"gf{k}_{i}", sib)

    def plane_copy(i, kind):
        to = (((x + i // 8) % 4) * 2 + yh) * 8 + (z + i % 8) % 8
        return pltpu.make_async_remote_copy(
            src_ref=msg.at[kind], dst_ref=plane.at[kind, i], send_sem=asend.at[kind, i], recv_sem=arecv.at[kind, i],
            device_id={"dp": to, "tensor": t}, device_id_type=MESH,
        )

    def line_copy(i, kind):
        q = (me + i) % 16
        to = (x * 2 + q // 8) * 8 + z
        return pltpu.make_async_remote_copy(
            src_ref=bmsg.at[kind], dst_ref=ball.at[kind, me], send_sem=bsend.at[kind, i], recv_sem=brecv.at[kind, me],
            device_id={"dp": to, "tensor": q % 8}, device_id_type=MESH,
        )

    def over(n, what):
        def step(i, _):
            what(i)
            return 0

        lax.fori_loop(1, n, step, 0)

    def merge(blocks):
        n = sum(jnp.broadcast_to(b[6:7, :], (8, 128)) for b in blocks)
        mean = sum(jnp.broadcast_to(b[6:7, :], (8, 128)) * b for b in blocks) / jnp.maximum(n, 1.0)
        apart = sum(jnp.broadcast_to(b[6:7, :], (8, 128)) * (b - mean) ** 2 for b in blocks)
        return n, mean, sum(blocks) + pltpu.roll(apart, 3, 0)

    row = lax.broadcasted_iota(jnp.int32, (8, 128), 0)

    def send_plane(kind):
        over(32, lambda i: plane_copy(i, kind).start())
        plane[kind, 0] = msg[kind]

    def plane_to_line(kind):
        over(32, lambda i: plane_copy(i, kind).wait_recv())
        n, mean, square = merge([plane[kind, i] for i in range(32)])
        bmsg[kind] = jnp.where(row < 3, mean, jnp.where(row == 6, n, square))
        over(16, lambda i: line_copy(i, kind).start())
        ball[kind, me] = bmsg[kind]

    for p in range(2):
        @pl.when(jnp.logical_not(mine & (c == p)))
        def _(p=p):
            for i in range(LNS):
                first = HALO + ROWS * p + LROWS * i
                arrived(nbuf.at[first : first + LROWS], f"blk{p}_{i}")

    @pl.when(((c == 1) & (j == 1)) | ((c == 0) & (h == 1)))
    def _():
        arrived(low, "low")

    @pl.when(((c == 0) & (j == 0)) | ((c == 1) & (h == 0)))
    def _():
        arrived(high, "high")

    loads[6].wait()
    arrived(wg.at[h, :, pl.ds(pl.multiple_of(SHARD * (1 - c), 64), SHARD)], "glu_sib")

    send(w_mine, w_quarter(t, colour), "wp", par_t)
    send(out_w, w_rows(t), "w_sib", sib)

    w_from = {"e": ext_t, "p": par_t, "q": pe_t}

    def w_on(s):
        at = w_quarter(w_from[s], colour)
        arrived(at, f"w{s}")
        if s == "e":
            send(at, at, "wq", par_t)
        for to_dp, _, k in near:
            send(at, at, f"w{s}x{k}", t, to_dp)
        send(at, at, f"w{s}f3", sib)

    def w_last(s):
        for k, (_, their, _) in enumerate(near):
            at = w_quarter(w_from[s], their)
            arrived(at, f"w{s}x{k}")
            send(at, at, f"w{s}f{k}", sib)

    one_tile(h, 0, 0)
    pass_glu(0)
    arrived(pack.at[2], "pack_e")
    send(pack.at[2], pack.at[3], "pack_d", sib)
    one_tile(h, 1, 0)
    pass_glu(1)
    w_on("e")
    one_tile(h, 2, 0)
    pass_glu(2)
    send_plane(0)
    give(h, 0, 3, 0)

    arrived(pack.at[3], "pack_d")
    tiles_of(1 - h, 2, 3)
    quarters = [their for _, their, _ in near] + [colour]
    for i in range(CHUNKS):
        for k in range(4):
            arrived(glu_rows(1 - h, 1 - c, quarters[k], i), f"gf{k}_{i}")
    one_tile(1 - h, 0, 1)
    one_tile(1 - h, 1, 1)
    give(1 - h, 0, 1, 1)
    one_tile(1 - h, 2, 1)
    send_plane(1)
    give(1 - h, 1, 2, 2)
    u = jnp.where(edge, 0, 1)
    for g in range(2):
        for s in range(2):
            send(mlm, mlx.at[s], f"ml{s}", owner + g, cond=jnp.logical_not(mine & (c == g)) & (u == s))

    @pl.when(mine)
    def _():
        mlx[u] = mlm[...]

    w_on("p")
    gmsg[...] = jnp.zeros_like(gmsg)
    for k in range(6):
        gmsg[k : k + 1, :] = par[k, TAPS : TAPS + 1, :]
        gmsg[8 + k : 9 + k, :] = par[k, TAPS + 1 : TAPS + 2, :]
    for giver in range(2):
        is_giver = t == 2 * giver
        for i in range(1, 8):
            send(gmsg, gall.at[giver], f"gain{giver}", (t + i) % 8, cond=is_giver)

        @pl.when(is_giver)
        def _(giver=giver):
            gall[giver] = gmsg[...]

    plane_to_line(0)
    w_on("q")
    w_last("e")
    plane_to_line(1)
    w_last("p")
    w_last("q")

    def line_arrived(i):
        q = (me + i) % 16
        for kind in range(2):
            pltpu.make_async_remote_copy(
                src_ref=bmsg.at[kind], dst_ref=ball.at[kind, q], send_sem=bsend.at[0, 0], recv_sem=brecv.at[kind, q],
                device_id={"dp": dp, "tensor": sib}, device_id_type=MESH,
            ).wait_recv()

    for group, n in ((0, 3), (1, 1), (2, 2)):
        for s in range(2):
            @pl.when(jnp.logical_not((j == s) & mine))
            def _(group=group, n=n, s=s):
                arrived(dbuf.at[pl.ds(0, n)], f"d{group}_{s}")
    for s in range(2):
        @pl.when(jnp.logical_not((u == s) & mine))
        def _(s=s):
            arrived(mlx.at[s], f"ml{s}")

    for giver in range(2):
        @pl.when(t != 2 * giver)
        def _(giver=giver):
            arrived(gall.at[giver], f"gain{giver}")

    over(16, line_arrived)
    for shard in range(4):
        from_own = [ball[0, 8 * g + 2 * shard + core] for g in range(2) for core in range(2)]
        from_extra = [ball[1, 8 * g + 2 * (3 - shard) + core] for g in range(2) for core in range(2)]
        n, mean, square = merge(from_own + from_extra)
        n1 = jnp.broadcast_to(n[0:1, :], (8, 128))
        pair = (0, 1, 1, 0)[shard]
        first = 3 * (shard // 2)
        root = lax.rsqrt(square / n1 + 1e-05)
        for r in range(3):
            g = 3 * shard + r
            k = first + r
            scale = root[3 + r : 4 + r, :] * gall[pair, k : k + 1, :]
            offset = mlx[pair, k : k + 1, :] - mean[r : r + 1, :]
            zed = (dbuf[g].astype(F32) + offset) * scale + gall[pair, 8 + k : 9 + k, :]
            act[:, 128 * g : 128 * (g + 1)] = (zed * jax.nn.sigmoid(zed)).astype(BF16)

    loads[7].wait()
    arrived(w_rows(sib), "w_sib")
    for s in "epq":
        for k in range(4):
            arrived(w_quarter(w_from[s] + 1 - 2 * c, quarters[k]), f"w{s}f{k}")

    def columns(i, _):
        at = pl.multiple_of(256 * i, 256)
        branch = lax.dot_general(
            act[...], wf[pl.ds(at, 256), :], (((1,), (1,)), ((), ())), preferred_element_type=F32
        )
        out[0, :, pl.ds(at, 256)] = (xin[:, pl.ds(at, 256)].astype(F32) + branch).astype(BF16)
        return 0

    lax.fori_loop(0, D // 256, columns, 0)

    for cond, copy in sent:
        if cond is None:
            copy.wait_send()
        else:
            pl.when(cond)(copy.wait_send)

    for kind in range(2):
        over(32, lambda i, kind=kind: plane_copy(i, kind).wait_send())
        over(16, lambda i, kind=kind: line_copy(i, kind).wait_send())


def per_device(
    frames_in, lengths, ln_gain, ln_bias, glu_weight, conv_kernel, bn_gain, bn_bias, out_weight
):
    hbm = pl.BlockSpec(memory_space=pltpu.HBM)
    dma = pltpu.SemaphoreType.DMA
    return pl.pallas_call(
        body,
        out_shape=jax.ShapeDtypeStruct((1, ROWS, D), BF16),
        in_specs=[hbm, pl.BlockSpec(memory_space=pltpu.SMEM)] + [hbm] * 7,
        out_specs=pl.BlockSpec(memory_space=pltpu.VMEM),
        scratch_shapes=[
            pltpu.VMEM((ROWS, D), BF16),
            pltpu.VMEM((D,), F32),
            pltpu.VMEM((D,), F32),
            pltpu.VMEM((TAPS, SHARD), BF16),
            pltpu.VMEM((SHARD,), F32),
            pltpu.VMEM((SHARD,), F32),
            pltpu.VMEM((ROWS, D), BF16),
            pltpu.VMEM((WIN, D), BF16),
            pltpu.VMEM((2, 2, CHIP, D), BF16),
            pltpu.VMEM((D, D), BF16),
            pltpu.VMEM((4, 40, 256), F32),
            pltpu.VMEM((6, 40, 128), F32),
            pltpu.VMEM((WIN, 128), F32),
            pltpu.VMEM((SPAN, 128), F32),
            pltpu.VMEM((6, SPAN, 128), BF16),
            pltpu.VMEM((12, ROWS, 128), BF16),
            pltpu.VMEM((2, 8, 128), F32),
            pltpu.VMEM((2, 32, 8, 128), F32),
            pltpu.VMEM((2, 8, 128), F32),
            pltpu.VMEM((16, 128), F32),
            pltpu.VMEM((2, 16, 8, 128), F32),
            pltpu.VMEM((2, 16, 128), F32),
            pltpu.VMEM((2, 8, 128), F32),
            pltpu.VMEM((8, 128), F32),
            pltpu.VMEM((ROWS, D), BF16),
            dma((9,)),
            dma((SENDS,)),
            dma((len(NAMES),)),
            dma((2, 32)),
            dma((2, 32)),
            dma((2, 16)),
            dma((2, 16)),
        ],
        compiler_params=pltpu.CompilerParams(
            collective_id=0, has_side_effects=True, vmem_limit_bytes=(64 << 20) - (128 << 10)
        ),
    )(
        frames_in, lengths, ln_gain, ln_bias, glu_weight, conv_kernel,
        bn_gain, bn_bias, out_weight,
    )


def solution(mesh):
    return jax.shard_map(
        per_device,
        mesh=mesh,
        in_specs=(
            P("dp", "tensor", None),
            P("dp"),
            P(),
            P(),
            P(None, "tensor", None),
            P(None, "tensor"),
            P("tensor"),
            P("tensor"),
            P("tensor", None),
        ),
        out_specs=P("dp", "tensor", None),
        check_vma=False,
    )
```

time: 68.5 us -> 58.8 us (0.86)
  Pallas kernels: 65.9 us -> 56.2 us
    pallas_call x1, Pallas kernels: 65.9 us -> 56.2 us  [per_device(): pl.pallas_call(body, out_shape=jax.ShapeDtypeStruct((1, ROWS, D), BF16),...]
where the time goes in v3:
time: 58.8 us; the launch traced here: 58.6 us
  Pallas kernels  56.2 us (96%)
  local copies, waits for them, and re-layouts  1.77 us (3%)
  between operations  0.66 us (1%)
    pallas_call x1, Pallas kernels, per_device(): pl.pallas_call(body, out_shape=jax.ShapeDtypeStruct((1, ROWS, D), BF16),...  56.2 us
    unnamed x1, local copies, waits for them, and re-layouts  1.77 us

profile of v3, /device:TPU:1, one launch (start us, length us, event | category | flops | bytes accessed | tf_op | source)
XLA Modules:
  0.0 58.6 jit_solution(3792794589065765718)
XLA Ops:
  0.7 56.2 %shard_map.91 = bf16[1,128,1536]{2,1,0:T(8,128)(2,1)} custom-call(bf16[1,128,1536]{2,1,0:T(8,128)(2,1)} %frames.1, s32[1]{0:T(128)S(6)} %copy.11.lengths, f32[1536]{0:T(1024)} %ln_gain.1, f32[1536]{0:T(1024)} %ln_bias.1, bf16[2,192,1536]{2,1,0:T(8,128)(2,1)} %glu_w.1, bf16[32,192]{1,0:T(8,128)(2,1)} %taps_in.1, f32[192]{0:T(256)} %bn_gain.1, f32[192]{0:T(256)} %bn_bias.1, ...), custom_call_target="tpu_custom_call" | custom-call | tf_op jit(solution)/shard_map/pallas_call | solution.py:491
  56.9 1.8 %copy.12 = bf16[1,128,1536]{2,1,0:T(8,128)(2,1)} copy(bf16[1,128,1536]{2,1,0:T(8,128)(2,1)} %shard_map.91) | data formatting | bytes 786432

commit v4 on v3

--- a/solution.py
+++ b/solution.py
@@ -21,7 +21,7 @@
 QUARTER = SHARD // 4
 CHUNKS = 3
 CROWS = QUARTER // CHUNKS
-LNS = 4
+LNS = 2
 LROWS = ROWS // LNS
 SENDS = 160
 
@@ -34,7 +34,7 @@
     + ["we", "wp", "wq"]
     + [f"w{s}x{k}" for s in "epq" for k in range(3)]
     + [f"w{s}f{k}" for s in "epq" for k in range(4)]
-    + [f"d{k}_{g}" for k in range(3) for g in range(2)]
+    + [f"d{k}_{g}" for k in range(2) for g in range(2)]
     + ["ml0", "ml1"]
     + ["gain0", "gain1"]
 )
@@ -115,32 +115,8 @@
     lax.fori_loop(1, 16, greet_line, 0)
     lax.fori_loop(1, 32, greet_plane, 0)
 
-    pl.semaphore_wait(barrier, 46)
-
-    same = (y + 2 * c - 1) // 2 == h
-    gives = ((c == 1) & (y < 3)) | ((c == 0) & (y > 0))
-    y2 = y + 2 * c - 1
-    h2, j2 = y2 // 2, (y2 + 2) % 2
-    mine = j == c
-
-    def glu_rows(slot, core, quarter, i):
-        first = SHARD * core + QUARTER * quarter + CROWS * i
-        return wg.at[slot, :, pl.ds(pl.multiple_of(first, 16), CROWS)]
-
-    def w_rows(shard, first=0, n=SHARD):
-        return wf.at[pl.ds(pl.multiple_of(SHARD * shard + first, 16), n)]
-
-    def w_quarter(shard, quarter):
-        return w_rows(shard, QUARTER * quarter, QUARTER)
-
-    for i in range(CHUNKS):
-        src = glu_w.at[:, pl.ds(pl.multiple_of(QUARTER * colour + CROWS * i, 16), CROWS)]
-        send(src, glu_rows(h, c, colour, i), f"gy{i}", ext_t, ext_dp)
-    send(glu_w, wg.at[h, :, pl.ds(pl.multiple_of(SHARD * c, 64), SHARD)], "glu_sib", sib)
-
     for copy in loads[:3]:
         copy.wait()
-    away = jnp.logical_not(mine)
     for i in range(LNS):
         at = slice(LROWS * i, LROWS * (i + 1))
         rows = xin[at, :].astype(F32)
@@ -149,6 +125,33 @@
         own[at, :] = (
             (rows - center) * lax.rsqrt(spread + 1e-05) * lng[...][None, :] + lnb[...][None, :]
         ).astype(BF16)
+    pl.semaphore_wait(barrier, 46)
+
+    same = (y + 2 * c - 1) // 2 == h
+    gives = ((c == 1) & (y < 3)) | ((c == 0) & (y > 0))
+    y2 = y + 2 * c - 1
+    h2, j2 = y2 // 2, (y2 + 2) % 2
+    mine = j == c
+
+    def glu_rows(slot, core, quarter, i):
+        first = SHARD * core + 64 * jnp.where(core == 0, i, 2 - i) + CROWS * quarter
+        return wg.at[slot, :, pl.ds(pl.multiple_of(first, 16), CROWS)]
+
+    def w_rows(shard, first=0, n=SHARD):
+        return wf.at[pl.ds(pl.multiple_of(SHARD * shard + first, 16), n)]
+
+    def w_quarter(shard, quarter):
+        return w_rows(shard, QUARTER * quarter, QUARTER)
+
+    for i in range(CHUNKS):
+        first = 64 * jnp.where(c == 0, i, 2 - i) + CROWS * colour
+        src = glu_w.at[:, pl.ds(pl.multiple_of(first, 16), CROWS)]
+        send(src, glu_rows(h, c, colour, i), f"gy{i}", ext_t, ext_dp)
+    send(glu_w, wg.at[h, :, pl.ds(pl.multiple_of(SHARD * c, 64), SHARD)], "glu_sib", sib)
+
+    away = jnp.logical_not(mine)
+    for i in range(LNS):
+        at = slice(LROWS * i, LROWS * (i + 1))
         spot = nbuf.at[pl.ds(pl.multiple_of(HALO + ROWS * c + LROWS * i, 16), LROWS)]
         for core in range(2):
             send(own.at[at], spot, f"blk{core}_{i}", (y + 1 - 2 * j) * 2 + j, cond=c == core)
@@ -298,12 +301,9 @@
             device_id={"dp": to, "tensor": q % 8}, device_id_type=MESH,
         )
 
-    def over(n, what):
-        def step(i, _):
+    def over(order, what):
+        for i in order:
             what(i)
-            return 0
-
-        lax.fori_loop(1, n, step, 0)
 
     def merge(blocks):
         n = sum(jnp.broadcast_to(b[6:7, :], (8, 128)) for b in blocks)
@@ -312,16 +312,18 @@
         return n, mean, sum(blocks) + pltpu.roll(apart, 3, 0)
 
     row = lax.broadcasted_iota(jnp.int32, (8, 128), 0)
+    plane_order = sorted(range(1, 32), key=lambda i: -min(i // 8, 4 - i // 8) - min(i % 8, 8 - i % 8))
+    line_order = sorted(range(1, 16), key=lambda i: -min(i, 16 - i))
 
     def send_plane(kind):
-        over(32, lambda i: plane_copy(i, kind).start())
+        over(plane_order, lambda i: plane_copy(i, kind).start())
         plane[kind, 0] = msg[kind]
 
     def plane_to_line(kind):
-        over(32, lambda i: plane_copy(i, kind).wait_recv())
+        over(plane_order, lambda i: plane_copy(i, kind).wait_recv())
         n, mean, square = merge([plane[kind, i] for i in range(32)])
         bmsg[kind] = jnp.where(row < 3, mean, jnp.where(row == 6, n, square))
-        over(16, lambda i: line_copy(i, kind).start())
+        over(line_order, lambda i: line_copy(i, kind).start())
         ball[kind, me] = bmsg[kind]
 
     for p in range(2):
@@ -364,11 +366,11 @@
 
     one_tile(h, 0, 0)
     pass_glu(0)
+    w_on("e")
     arrived(pack.at[2], "pack_e")
     send(pack.at[2], pack.at[3], "pack_d", sib)
     one_tile(h, 1, 0)
     pass_glu(1)
-    w_on("e")
     one_tile(h, 2, 0)
     pass_glu(2)
     send_plane(0)
@@ -377,15 +379,19 @@
     arrived(pack.at[3], "pack_d")
     tiles_of(1 - h, 2, 3)
     quarters = [their for _, their, _ in near] + [colour]
-    for i in range(CHUNKS):
+
+    def glu_arrived(i):
         for k in range(4):
             arrived(glu_rows(1 - h, 1 - c, quarters[k], i), f"gf{k}_{i}")
+
+    glu_arrived(0)
+    glu_arrived(1)
     one_tile(1 - h, 0, 1)
+    one_tile(1 - h, 2, 1)
+    glu_arrived(2)
     one_tile(1 - h, 1, 1)
-    give(1 - h, 0, 1, 1)
-    one_tile(1 - h, 2, 1)
     send_plane(1)
-    give(1 - h, 1, 2, 2)
+    give(1 - h, 0, 3, 1)
     u = jnp.where(edge, 0, 1)
     for g in range(2):
         for s in range(2):
@@ -395,7 +401,6 @@
     def _():
         mlx[u] = mlm[...]
 
-    w_on("p")
     gmsg[...] = jnp.zeros_like(gmsg)
     for k in range(6):
         gmsg[k : k + 1, :] = par[k, TAPS : TAPS + 1, :]
@@ -409,10 +414,11 @@
         def _(giver=giver):
             gall[giver] = gmsg[...]
 
+    w_last("e")
     plane_to_line(0)
+    w_on("p")
+    plane_to_line(1)
     w_on("q")
-    w_last("e")
-    plane_to_line(1)
     w_last("p")
     w_last("q")
 
@@ -424,7 +430,7 @@
                 device_id={"dp": dp, "tensor": sib}, device_id_type=MESH,
             ).wait_recv()
 
-    for group, n in ((0, 3), (1, 1), (2, 2)):
+    for group, n in ((0, 3), (1, 3)):
         for s in range(2):
             @pl.when(jnp.logical_not((j == s) & mine))
             def _(group=group, n=n, s=s):
@@ -439,7 +445,7 @@
         def _(giver=giver):
             arrived(gall.at[giver], f"gain{giver}")
 
-    over(16, line_arrived)
+    over(line_order, line_arrived)
     for shard in range(4):
         from_own = [ball[0, 8 * g + 2 * shard + core] for g in range(2) for core in range(2)]
         from_extra = [ball[1, 8 * g + 2 * (3 - shard) + core] for g in range(2) for core in range(2)]
@@ -456,21 +462,20 @@
             zed = (dbuf[g].astype(F32) + offset) * scale + gall[pair, 8 + k : 9 + k, :]
             act[:, 128 * g : 128 * (g + 1)] = (zed * jax.nn.sigmoid(zed)).astype(BF16)
 
+    def columns(chip):
+        at = pl.multiple_of(CHIP * chip, 128)
+        branch = lax.dot_general(
+            act[...], wf[pl.ds(at, CHIP), :], (((1,), (1,)), ((), ())), preferred_element_type=F32
+        )
+        out[0, :, pl.ds(at, CHIP)] = (xin[:, pl.ds(at, CHIP)].astype(F32) + branch).astype(BF16)
+
     loads[7].wait()
     arrived(w_rows(sib), "w_sib")
+    columns(y)
     for s in "epq":
         for k in range(4):
             arrived(w_quarter(w_from[s] + 1 - 2 * c, quarters[k]), f"w{s}f{k}")
-
-    def columns(i, _):
-        at = pl.multiple_of(256 * i, 256)
-        branch = lax.dot_general(
-            act[...], wf[pl.ds(at, 256), :], (((1,), (1,)), ((), ())), preferred_element_type=F32
-        )
-        out[0, :, pl.ds(at, 256)] = (xin[:, pl.ds(at, 256)].astype(F32) + branch).astype(BF16)
-        return 0
-
-    lax.fori_loop(0, D // 256, columns, 0)
+        columns(w_from[s] // 2)
 
     for cond, copy in sent:
         if cond is None:
@@ -479,8 +484,8 @@
             pl.when(cond)(copy.wait_send)
 
     for kind in range(2):
-        over(32, lambda i, kind=kind: plane_copy(i, kind).wait_send())
-        over(16, lambda i, kind=kind: line_copy(i, kind).wait_send())
+        over(plane_order, lambda i, kind=kind: plane_copy(i, kind).wait_send())
+        over(line_order, lambda i, kind=kind: line_copy(i, kind).wait_send())
 
 
 def per_device(
@@ -488,6 +493,7 @@
 ):
     hbm = pl.BlockSpec(memory_space=pltpu.HBM)
     dma = pltpu.SemaphoreType.DMA
+    far = functools.partial(pltpu.with_memory_space_constraint, memory_space=pltpu.HBM)
     return pl.pallas_call(
         body,
         out_shape=jax.ShapeDtypeStruct((1, ROWS, D), BF16),
@@ -528,11 +534,11 @@
             dma((2, 16)),
         ],
         compiler_params=pltpu.CompilerParams(
-            collective_id=0, has_side_effects=True, vmem_limit_bytes=(64 << 20) - (128 << 10)
+            collective_id=0, has_side_effects=True, vmem_limit_bytes=48 << 20
         ),
     )(
-        frames_in, lengths, ln_gain, ln_bias, glu_weight, conv_kernel,
-        bn_gain, bn_bias, out_weight,
+        far(frames_in), lengths, far(ln_gain), far(ln_bias), far(glu_weight), far(conv_kernel),
+        far(bn_gain), far(bn_bias), far(out_weight),
     )
 
 

time: 58.8 us -> 55.1 us (0.937)
  Pallas kernels: 56.2 us -> 53.6 us
  local copies, waits for them, and re-layouts: 1.77 us -> 0.75 us
    pallas_call x1, Pallas kernels: 56.2 us -> 53.6 us  [per_device(): pl.pallas_call(body, out_shape=jax.ShapeDtypeStruct((1, ROWS, D), BF16),...]
    unnamed x1, local copies, waits for them, and re-layouts: 1.77 us -> 0.75 us
where the time goes in v4:
time: 55.1 us; the launch traced here: 55 us
  Pallas kernels  53.6 us (97%)
  local copies, waits for them, and re-layouts  0.75 us (1%)
  between operations  0.66 us (1%)
    pallas_call x1, Pallas kernels, per_device(): pl.pallas_call(body, out_shape=jax.ShapeDtypeStruct((1, ROWS, D), BF16),...  53.6 us

profile of v4, /device:TPU:1, one launch (start us, length us, event | category | flops | bytes accessed | tf_op | source)
XLA Modules:
  0.0 55.0 jit_solution(14917758571425814208)
XLA Ops:
  0.7 53.6 %shard_map.91 = bf16[1,128,1536]{2,1,0:T(8,128)(2,1)S(1)} custom-call(bf16[1,128,1536]{2,1,0:T(8,128)(2,1)} %frames.1, s32[1]{0:T(128)S(6)} %copy.11.lengths, f32[1536]{0:T(1024)} %ln_gain.1, f32[1536]{0:T(1024)} %ln_bias.1, bf16[2,192,1536]{2,1,0:T(8,128)(2,1)} %glu_w.1, bf16[32,192]{1,0:T(8,128)(2,1)} %taps_in.1, f32[192]{0:T(256)} %bn_gain.1, ...), custom_call_target="tpu_custom_call" | custom-call | tf_op jit(solution)/shard_map/pallas_call | solution.py:497
  54.2 0.7 %copy.12 = bf16[1,128,1536]{2,1,0:T(8,128)(2,1)} copy(bf16[1,128,1536]{2,1,0:T(8,128)(2,1)S(1)} %shard_map.91) | data formatting | bytes 786432

commit v5 on v4

--- a/solution.py
+++ b/solution.py
@@ -230,7 +230,7 @@
         glu = (both[:, 0:128] * jax.nn.sigmoid(both[:, 128:256])).astype(BF16).astype(F32)
         at = lax.broadcasted_iota(jnp.int32, (WIN, 128), 0)
         gs[...] = jnp.where(at < length - start + HALO, glu, 0.0)
-        step = 64
+        step = 128
 
         def conv_rows(i, total):
             first = pl.multiple_of(i * step, step)
@@ -414,9 +414,9 @@
         def _(giver=giver):
             gall[giver] = gmsg[...]
 
-    w_last("e")
     plane_to_line(0)
     w_on("p")
+    w_last("e")
     plane_to_line(1)
     w_on("q")
     w_last("p")

time: 55.1 us -> 54.9 us (level)
  no operation moved by 1% of the time
where the time goes in v5:
time: 54.9 us; the launch traced here: 54.8 us
  Pallas kernels  53.4 us (97%)
  local copies, waits for them, and re-layouts  0.75 us (1%)
  between operations  0.66 us (1%)
    pallas_call x1, Pallas kernels, per_device(): pl.pallas_call(body, out_shape=jax.ShapeDtypeStruct((1, ROWS, D), BF16),...  53.4 us

profile of v5, /device:TPU:1, one launch (start us, length us, event | category | flops | bytes accessed | tf_op | source)
XLA Modules:
  0.0 54.8 jit_solution(6113641172621956399)
XLA Ops:
  0.7 53.4 %shard_map.91 = bf16[1,128,1536]{2,1,0:T(8,128)(2,1)S(1)} custom-call(bf16[1,128,1536]{2,1,0:T(8,128)(2,1)} %frames.1, s32[1]{0:T(128)S(6)} %copy.11.lengths, f32[1536]{0:T(1024)} %ln_gain.1, f32[1536]{0:T(1024)} %ln_bias.1, bf16[2,192,1536]{2,1,0:T(8,128)(2,1)} %glu_w.1, bf16[32,192]{1,0:T(8,128)(2,1)} %taps_in.1, f32[192]{0:T(256)} %bn_gain.1, ...), custom_call_target="tpu_custom_call" | custom-call | tf_op jit(solution)/shard_map/pallas_call | solution.py:497
  54.0 0.7 %copy.12 = bf16[1,128,1536]{2,1,0:T(8,128)(2,1)} copy(bf16[1,128,1536]{2,1,0:T(8,128)(2,1)S(1)} %shard_map.91) | data formatting | bytes 786432
